TPU v7x, 128 devices: a whole 4x4x4 slice. The times are simulated.
128 devices in a mesh: row: 8 (over y, core), col: 16 (over x, z).
Axes of the slice: x: 4, y: 4, z: 4, core: 2. Of those that a mesh axis runs over, the one named last changes fastest.
Arguments:
- probes: bfloat16 [4, 32768, 256], P(None, ('row', 'col')), may hold values from -6 to 6
- points: bfloat16 [16, 4, 32768], P(None, None, ('row', 'col')), may hold values from -8 to 8
- leaf_skeleton: int32 [256, 64], P(('row', 'col')), may hold values from 0 to 127, as said below
- skeleton_one: int32 [128, 64], P(('row', 'col')), may hold values from 0 to 127, as said below
- skeleton_two: int32 [64, 64], P('row'), may hold values from 0 to 127, as said below
- skeleton_three: int32 [32, 64], P('row'), may hold values from 0 to 127, as said below
Outputs:
- leaf_interp: float32 [256, 128, 64], P(('row', 'col'))
- upper_interp: float32 [3, 128, 128, 64], P(None, ('row', 'col'))
- top_state: float32 [2, 128, 64, 256], P(None, ('row', 'col'))
Inputs may be any that keep to these rules, and one draw needn't show every extreme that they name: `leaf_skeleton`: each row names 64 different rows of its leaf, in ascending order. `skeleton_one`: each row names 64 different rows of the node's stacked child skeletons, in ascending order. `skeleton_two`: each row names 64 different rows of the node's stacked child skeletons, in ascending order. `skeleton_three`: each row names 64 different rows of the node's stacked child skeletons, in ascending order.
All inputs are finite; a program needn't handle non-finite values.
Results may differ from a plain program's by a relative error of at most 0.0059.
Values may be sent and summed in bfloat16 or wider, within the bound.
A program may use at most 64 MiB of HBM per device.

v0:
```python
from functools import partial
import math

import jax
import jax.numpy as jnp
from jax import lax
from jax.sharding import PartitionSpec as P

LEAF = 128


exact_mode = lax.Precision.HIGHEST


def swapped(value, axis, bit):
    return lax.ppermute(value, axis, [(i, i ^ 1 << bit) for i in range(lax.axis_size(axis))])


def couple(row_feats, col_feats, kernel_gain):
    cross = jnp.dot(row_feats.T, col_feats, precision=exact_mode)
    row_sq = jnp.sum(row_feats * row_feats, axis=0)
    col_sq = jnp.sum(col_feats * col_feats, axis=0)
    feat_count = row_feats.shape[0]
    return kernel_gain * jnp.exp(
        (2.0 * cross - row_sq[:, None] - col_sq[None, :]) / (2.0 * feat_count)
    )


def interpolate(stacked, chosen):
    skeleton = jnp.take(stacked, chosen, axis=0)
    gram_mat = jnp.dot(skeleton, skeleton.T, precision=exact_mode)
    damping = 0.05 * jnp.sum(skeleton * skeleton) / chosen.shape[0] + 1e-05
    factor = jnp.linalg.cholesky(gram_mat + damping * jnp.eye(chosen.shape[0], dtype=stacked.dtype))
    cross_mat = jnp.dot(stacked, skeleton.T, precision=exact_mode)
    solved = jax.scipy.linalg.cho_solve((factor, True), cross_mat.T)
    return (solved.T, skeleton)


def leaf_level(leaf_rows, leaf_probes, coords, chosen):
    interp, skeleton = interpolate(leaf_rows, chosen)
    reduced = jnp.dot(interp.T, leaf_probes.astype(interp.dtype), precision=exact_mode)
    picked = jnp.take(coords, chosen, axis=1).astype(jnp.float32)
    return (interp, (skeleton, reduced, picked))


def merge_pair(first_child, second_child, chosen, kernel_gain):
    first_samples, first_reduced, first_points = first_child
    second_samples, second_reduced, second_points = second_child
    upper_rows = first_samples - jnp.dot(
        couple(first_points, second_points, kernel_gain), second_reduced, precision=exact_mode
    )
    lower_rows = second_samples - jnp.dot(
        couple(second_points, first_points, kernel_gain), first_reduced, precision=exact_mode
    )
    stacked = jnp.concatenate([upper_rows, lower_rows], axis=0)
    interp, skeleton = interpolate(stacked, chosen)
    reduced = jnp.dot(
        interp.T, jnp.concatenate([first_reduced, second_reduced], axis=0), precision=exact_mode
    )
    joined = jnp.take(jnp.concatenate([first_points, second_points], axis=1), chosen, axis=1)
    return (interp, (skeleton, reduced, joined))


def take_first(values):
    return values[0]


def take_second(values):
    return values[1]


def local(probes, points, leaf_skeleton, skeleton_one, skeleton_two, skeleton_three):
    feat_count = points.shape[0]
    own_rows = probes.shape[1]
    row_count = lax.axis_size("row")
    col_count = lax.axis_size("col")
    row_pos = lax.axis_index("row")
    col_pos = lax.axis_index("col")
    row_span = own_rows * col_count
    extent = row_span * row_count
    kernel_gain = 16.0 / math.sqrt(4 * extent)
    probe_cols = lax.all_gather(probes, "row", axis=1, tiled=True).reshape(
        4 * row_count * own_rows, -1
    )
    row_coords = lax.all_gather(points[:, 0], "col", axis=1, tiled=True)
    col_coords = lax.all_gather(points, "row", axis=2, tiled=True).reshape(
        feat_count, 4 * row_count * own_rows
    )
    col_wide = col_coords.astype(jnp.float32)
    col_sq = jnp.sum(col_wide * col_wide, axis=0)
    row_leaf = (row_pos * row_span + jnp.arange(row_span, dtype=jnp.int32)) // LEAF
    quarter_len = row_count * own_rows
    offsets = jnp.arange(4 * quarter_len, dtype=jnp.int32)
    quarter = offsets // quarter_len
    within = offsets % quarter_len
    col_leaf = (
        quarter * extent + within // own_rows * row_span + col_pos * own_rows + within % own_rows
    ) // LEAF
    height = 512

    def one_block(first_row):
        coords = lax.dynamic_slice_in_dim(row_coords, first_row, height, 1)
        leaves = lax.dynamic_slice_in_dim(row_leaf, first_row, height, 0)
        cross = lax.dot_general(
            coords, col_coords, (((0,), (0,)), ((), ())), preferred_element_type=jnp.float32
        )
        row_wide = coords.astype(jnp.float32)
        row_sq = jnp.sum(row_wide * row_wide, axis=0)
        kernel_tile = kernel_gain * jnp.exp(
            (2.0 * cross - row_sq[:, None] - col_sq[None, :]) / (2.0 * feat_count)
        )
        kernel_tile = jnp.where(leaves[:, None] == col_leaf[None, :], 0.0, kernel_tile).astype(
            jnp.bfloat16
        )
        return jnp.dot(kernel_tile, probe_cols, preferred_element_type=jnp.float32)

    starts = jnp.arange(row_span // height, dtype=jnp.int32) * height
    summed = lax.psum(lax.map(one_block, starts).reshape(row_span, -1), "col")
    owned = lax.dynamic_slice_in_dim(summed, col_pos * own_rows, own_rows, 0)
    leaf_count = own_rows // LEAF
    leaf_rows = owned.reshape(leaf_count, LEAF, -1)
    leaf_probes = probes[0].reshape(leaf_count, LEAF, -1)
    leaf_coords = points[:, 0].reshape(feat_count, leaf_count, LEAF).transpose(1, 0, 2)
    leaf_interp, carried = jax.vmap(leaf_level)(leaf_rows, leaf_probes, leaf_coords, leaf_skeleton)
    first_child = jax.tree.map(take_first, carried)
    second_child = jax.tree.map(take_second, carried)
    interp_one, carried = merge_pair(first_child, second_child, skeleton_one[0], kernel_gain)
    upper_list = [interp_one]
    for bit_num in range(2):
        partner = swapped((carried[0], carried[1], carried[2]), "col", bit_num)
        mine_first = col_pos >> bit_num & 1 == 0
        first_child = jax.tree.map(partial(jnp.where, mine_first), carried, partner)
        second_child = jax.tree.map(partial(jnp.where, mine_first), partner, carried)
        table_rows = skeleton_two if bit_num == 0 else skeleton_three
        chosen = lax.dynamic_index_in_dim(table_rows, col_pos // (2 << bit_num), 0, keepdims=False)
        interp_up, carried = merge_pair(first_child, second_child, chosen, kernel_gain)
        upper_list.append(interp_up)
    upper_interp = jnp.stack(upper_list)[:, None]
    top_state = jnp.stack([carried[0], carried[1]])[:, None]
    return (leaf_interp, upper_interp, top_state)


def solution(mesh):
    placed = (
        P(None, ("row", "col"), None),
        P(None, None, ("row", "col")),
        P(("row", "col"), None),
        P(("row", "col"), None),
        P("row", None),
        P("row", None),
    )
    return jax.shard_map(
        local,
        mesh=mesh,
        in_specs=placed,
        out_specs=(
            P(("row", "col"), None, None),
            P(None, ("row", "col"), None, None),
            P(None, ("row", "col"), None, None),
        ),
        check_vma=False,
    )
```

profile of v0, /device:TPU:0, one launch (start us, length us, event | category | flops | bytes accessed | tf_op | source)
XLA Modules:
  0.0 333.6 jit_solution(17776641699340166567)
XLA Ops:
  8.7 12.7 %all_gather.10 = bf16[16,4,2048]{2,1,0:T(4,128)(2,1)S(1)} all-gather(bf16[16,4,256]{2,1,0:T(4,128)(2,1)} %param.16), channel_id=1, replica_groups=mesh['row'=8,'col'=16] {'row'}, dimensions={2}, use_global_device_ids=true | all-gather | bytes 294912 | tf_op jit(solution)/shard_map/all_gather | solution.py:86
  21.8 25.1 %all-gather = bf16[16,1,4096]{2,0,1:T(8,128)(2,1)S(1)} all-gather(bf16[16,1,256]{2,0,1:T(8,128)(2,1)S(1)} %copy.60), channel_id=2, replica_groups=mesh['row'=8,'col'=16] {'col'}, dimensions={2}, use_global_device_ids=true | all-gather | bytes 139264 | tf_op jit(solution)/shard_map/all_gather | solution.py:85
  46.9 88.3 %while.11 = (s32[]{:T(128)}, f32[8,512,256]{2,1,0:T(8,128)}, s32[8]{0:T(128)S(1)}, s32[4096]{0:T(1024)S(1)}, bf16[16,4096]{1,0:T(8,128)(2,1)S(1)}, /*index=5*/bf...) while((s32[]{:T(128)}, f32[8,512,256]{2,1,0:T(8,128)}, ...), condition=%wide.region_3.4_spmd.clone, body=%wide.region_1.3_spmd.clone.sunk | while | flops 2315697664 | bytes 5122239 | solution.py:118
  49.7 8.3 %fusion.176 = f32[8,512,256]{2,1,0:T(8,128)} fusion(f32[8,512,256]{2,1,0:T(8,128)} %get-tuple-element.213, s32[]{:T(128)S(6)} %copy.67, bf16[8192,256]{1,0:T(8,128)(2,1)} %get-tuple-element.231, bf16[16,8192]{1,0:T(8,128)(2,1)S(1)} %get-tuple-element.229, f32[8192]{0:T(1024)S(1)} %get-tuple-element.230, f32[512]{0:T(512)S(1)} %multiply_reduce_fusion.13, ...), kind=kOutput, calls=%fused_computation.11.clone.1 | convolution fusion | flops 2315255808 | bytes 5066760 | tf_op jit(solution)/shard_map/while/body/eval_jaxpr/dot_general | solution.py:115
  60.7 8.3 %fusion.176 = f32[8,512,256]{2,1,0:T(8,128)} fusion(f32[8,512,256]{2,1,0:T(8,128)} %get-tuple-element.213, s32[]{:T(128)S(6)} %copy.67, bf16[8192,256]{1,0:T(8,128)(2,1)} %get-tuple-element.231, bf16[16,8192]{1,0:T(8,128)(2,1)S(1)} %get-tuple-element.229, f32[8192]{0:T(1024)S(1)} %get-tuple-element.230, f32[512]{0:T(512)S(1)} %multiply_reduce_fusion.13, ...), kind=kOutput, calls=%fused_computation.11.clone.1 | convolution fusion | flops 2315255808 | bytes 5066760 | tf_op jit(solution)/shard_map/while/body/eval_jaxpr/dot_general | solution.py:115
  71.8 8.3 %fusion.176 = f32[8,512,256]{2,1,0:T(8,128)} fusion(f32[8,512,256]{2,1,0:T(8,128)} %get-tuple-element.213, s32[]{:T(128)S(6)} %copy.67, bf16[8192,256]{1,0:T(8,128)(2,1)} %get-tuple-element.231, bf16[16,8192]{1,0:T(8,128)(2,1)S(1)} %get-tuple-element.229, f32[8192]{0:T(1024)S(1)} %get-tuple-element.230, f32[512]{0:T(512)S(1)} %multiply_reduce_fusion.13, ...), kind=kOutput, calls=%fused_computation.11.clone.1 | convolution fusion | flops 2315255808 | bytes 5066760 | tf_op jit(solution)/shard_map/while/body/eval_jaxpr/dot_general | solution.py:115
  82.8 8.3 %fusion.176 = f32[8,512,256]{2,1,0:T(8,128)} fusion(f32[8,512,256]{2,1,0:T(8,128)} %get-tuple-element.213, s32[]{:T(128)S(6)} %copy.67, bf16[8192,256]{1,0:T(8,128)(2,1)} %get-tuple-element.231, bf16[16,8192]{1,0:T(8,128)(2,1)S(1)} %get-tuple-element.229, f32[8192]{0:T(1024)S(1)} %get-tuple-element.230, f32[512]{0:T(512)S(1)} %multiply_reduce_fusion.13, ...), kind=kOutput, calls=%fused_computation.11.clone.1 | convolution fusion | flops 2315255808 | bytes 5066760 | tf_op jit(solution)/shard_map/while/body/eval_jaxpr/dot_general | solution.py:115
  93.9 8.3 %fusion.176 = f32[8,512,256]{2,1,0:T(8,128)} fusion(f32[8,512,256]{2,1,0:T(8,128)} %get-tuple-element.213, s32[]{:T(128)S(6)} %copy.67, bf16[8192,256]{1,0:T(8,128)(2,1)} %get-tuple-element.231, bf16[16,8192]{1,0:T(8,128)(2,1)S(1)} %get-tuple-element.229, f32[8192]{0:T(1024)S(1)} %get-tuple-element.230, f32[512]{0:T(512)S(1)} %multiply_reduce_fusion.13, ...), kind=kOutput, calls=%fused_computation.11.clone.1 | convolution fusion | flops 2315255808 | bytes 5066760 | tf_op jit(solution)/shard_map/while/body/eval_jaxpr/dot_general | solution.py:115
  104.9 8.3 %fusion.176 = f32[8,512,256]{2,1,0:T(8,128)} fusion(f32[8,512,256]{2,1,0:T(8,128)} %get-tuple-element.213, s32[]{:T(128)S(6)} %copy.67, bf16[8192,256]{1,0:T(8,128)(2,1)} %get-tuple-element.231, bf16[16,8192]{1,0:T(8,128)(2,1)S(1)} %get-tuple-element.229, f32[8192]{0:T(1024)S(1)} %get-tuple-element.230, f32[512]{0:T(512)S(1)} %multiply_reduce_fusion.13, ...), kind=kOutput, calls=%fused_computation.11.clone.1 | convolution fusion | flops 2315255808 | bytes 5066760 | tf_op jit(solution)/shard_map/while/body/eval_jaxpr/dot_general | solution.py:115
  116.0 8.3 %fusion.176 = f32[8,512,256]{2,1,0:T(8,128)} fusion(f32[8,512,256]{2,1,0:T(8,128)} %get-tuple-element.213, s32[]{:T(128)S(6)} %copy.67, bf16[8192,256]{1,0:T(8,128)(2,1)} %get-tuple-element.231, bf16[16,8192]{1,0:T(8,128)(2,1)S(1)} %get-tuple-element.229, f32[8192]{0:T(1024)S(1)} %get-tuple-element.230, f32[512]{0:T(512)S(1)} %multiply_reduce_fusion.13, ...), kind=kOutput, calls=%fused_computation.11.clone.1 | convolution fusion | flops 2315255808 | bytes 5066760 | tf_op jit(solution)/shard_map/while/body/eval_jaxpr/dot_general | solution.py:115
  127.0 8.3 %fusion.176 = f32[8,512,256]{2,1,0:T(8,128)} fusion(f32[8,512,256]{2,1,0:T(8,128)} %get-tuple-element.213, s32[]{:T(128)S(6)} %copy.67, bf16[8192,256]{1,0:T(8,128)(2,1)} %get-tuple-element.231, bf16[16,8192]{1,0:T(8,128)(2,1)S(1)} %get-tuple-element.229, f32[8192]{0:T(1024)S(1)} %get-tuple-element.230, f32[512]{0:T(512)S(1)} %multiply_reduce_fusion.13, ...), kind=kOutput, calls=%fused_computation.11.clone.1 | convolution fusion | flops 2315255808 | bytes 5066760 | tf_op jit(solution)/shard_map/while/body/eval_jaxpr/dot_general | solution.py:115
  136.2 1.1 gather_fusion.1
  138.3 1.3 collective-permute-start.1
  143.1 2.5 collective-permute-start.4
  146.1 3.6 %collective-permute-done.4 = f32[16,64]{0,1:T(8,128)S(1)} collective-permute-done((f32[16,64]{0,1:T(8,128)S(1)}, f32[16,64]{0,1:T(8,128)S(1)}, u32[]{:S(2)}, u32[]{:S(2)}) %collective-permute-start.4) | collective-permute-done | bytes 4128 | tf_op jit(solution)/shard_map/ppermute | solution.py:16
  149.8 87.9 %all-reduce.2.cloned.1.call-done = f32[4096,256]{1,0:T(8,128)} async-done(((f32[4096,256]{1,0:T(8,128)}), f32[4096,256]{1,0:T(8,128)}) %all-reduce.2.cloned.1.call-update) | async-done | bytes 4194320 | tf_op jit(solution)/shard_map/psum | solution.py:118
  237.7 1.0 constant_dynamic-slice_fusion.2
  238.7 1.3 gather_fusion
  241.0 11.7 %custom-call.18 = f32[2,64,64]{2,1,0:T(8,128)S(1)} custom-call(f32[2,64,64]{2,1,0:T(8,128)S(1)} %fusion.80), custom_call_target="Cholesky" | custom-call | tf_op jit(solution)/shard_map/vmap(jit(cholesky))/cholesky | solution.py:33
  253.0 9.8 %custom-call.19 = f32[2,1,64,64]{2,3,1,0:T(8,128)S(1)} custom-call(f32[2,1,64,64]{3,2,1,0:T(8,128)S(1)} %select_bitcast_fusion), custom_call_target="InvertDiagBlocksLowerTriangular" | custom-call | tf_op jit(solution)/shard_map/vmap(jit(_cho_solve))/triangular_solve | solution.py:35
  266.6 5.8 %cholesky.106 = f32[64,64]{1,0:T(8,128)S(1)} custom-call(f32[64,64]{1,0:T(8,128)S(1)} %fusion.101), custom_call_target="Cholesky" | custom-call | tf_op jit(solution)/shard_map/jit(cholesky)/cholesky | solution.py:33
  273.8 4.9 %custom-call.26 = f32[1,64,64]{1,2,0:T(8,128)S(1)} custom-call(f32[1,64,64]{2,1,0:T(8,128)S(1)} %fusion.84), custom_call_target="InvertDiagBlocksLowerTriangular" | custom-call | tf_op jit(solution)/shard_map/jit(_cho_solve)/triangular_solve | solution.py:35
  279.3 1.3 collective-permute-start.2
  281.7 2.5 collective-permute-done.2
  287.9 5.8 %cholesky.117 = f32[64,64]{1,0:T(8,128)S(1)} custom-call(f32[64,64]{1,0:T(8,128)S(1)} %fusion.96), custom_call_target="Cholesky" | custom-call | tf_op jit(solution)/shard_map/jit(cholesky)/cholesky | solution.py:33
  295.1 4.9 %custom-call.27 = f32[1,64,64]{1,2,0:T(8,128)S(1)} custom-call(f32[1,64,64]{2,1,0:T(8,128)S(1)} %fusion.85), custom_call_target="InvertDiagBlocksLowerTriangular" | custom-call | tf_op jit(solution)/shard_map/jit(_cho_solve)/triangular_solve | solution.py:35
  300.6 2.9 collective-permute-start.5
  303.8 1.0 collective-permute-start.3
  304.7 1.7 collective-permute-done.5
  306.7 3.1 collective-permute-done.3
  312.7 5.8 %cholesky.128 = f32[64,64]{1,0:T(8,128)S(1)} custom-call(f32[64,64]{1,0:T(8,128)S(1)} %fusion.91), custom_call_target="Cholesky" | custom-call | tf_op jit(solution)/shard_map/jit(cholesky)/cholesky | solution.py:33
  319.9 4.9 %custom-call.28 = f32[1,64,64]{1,2,0:T(8,128)S(1)} custom-call(f32[1,64,64]{2,1,0:T(8,128)S(1)} %fusion.86), custom_call_target="InvertDiagBlocksLowerTriangular" | custom-call | tf_op jit(solution)/shard_map/jit(_cho_solve)/triangular_solve | solution.py:35
  (152 shorter events, 32.3 us)
Async XLA Ops:
  7.2 39.8 %all-gather.3.cloned.1.call-start = ((), (), s32[]{:S(2)}) async-start(), calls=%async_computation | async-start | bytes 4718592 | tf_op jit(solution)/shard_map/all_gather | solution.py:82
  7.9 229.8 %all-reduce.2.cloned.1.call-start = ((), (), s32[]{:S(2)}) async-start(), calls=%async_computation.1 | async-start | bytes 8388608 | tf_op jit(solution)/shard_map/psum | solution.py:118
  135.3 0.7 copy-start.1
  135.3 2.3 copy-start.2
  138.3 4.0 %collective-permute-start.1 = (f32[16,64]{0,1:T(8,128)S(1)}, f32[16,64]{0,1:T(8,128)S(1)}, u32[]{:S(2)}, u32[]{:S(2)}) collective-permute-start(f32[16,64]{0,1:T(8,128)S(1)} %select_bitcast_fusion.3), channel_id=1, source_target_pairs={{0,1},{1,0},{2,3},{3,2},{4,5},{5,4},{6,7},{7,6},{8,9},{9,8},{10,11... | collective-permute-start | bytes 12296 | tf_op jit(solution)/shard_map/ppermute | solution.py:16
  143.1 6.5 %collective-permute-start.4 = (f32[16,64]{0,1:T(8,128)S(1)}, f32[16,64]{0,1:T(8,128)S(1)}, u32[]{:S(2)}, u32[]{:S(2)}) collective-permute-start(f32[16,64]{0,1:T(8,128)S(1)} %select_bitcast_fusion.2), channel_id=1, source_target_pairs={{0,2},{1,3},{2,0},{3,1},{4,6},{5,7},{6,4},{7,5},{8,10},{9,11},{10,... | collective-permute-start | bytes 12296 | tf_op jit(solution)/shard_map/ppermute | solution.py:16
  263.3 49.3 %copy-start = (f32[2,64,128]{2,1,0:T(8,128)}, f32[2,64,128]{2,1,0:T(8,128)S(1)}, u32[]{:S(2)}) copy-start(f32[2,64,128]{2,1,0:T(8,128)S(1)} %fusion.75) | copy-start | bytes 196612
  279.3 4.9 %collective-permute-start.2 = (f32[64,256]{1,0:T(8,128)S(1)}, f32[64,256]{1,0:T(8,128)S(1)}, u32[]{:S(2)}, u32[]{:S(2)}) collective-permute-start(f32[64,256]{1,0:T(8,128)S(1)} %fusion.64), channel_id=1, source_target_pairs={{0,1},{1,0},{2,3},{3,2},{4,5},{5,4},{6,7},{7,6},{8,9},{9,8},{10,11... | collective-permute-start | bytes 196616 | tf_op jit(solution)/shard_map/ppermute | solution.py:16
  280.8 4.3 %collective-permute-start = (f32[64,256]{1,0:T(8,128)S(1)}, f32[64,256]{1,0:T(8,128)S(1)}, u32[]{:S(2)}, u32[]{:S(2)}) collective-permute-start(f32[64,256]{1,0:T(8,128)S(1)} %get-tuple-element.110), channel_id=1, source_target_pairs={{0,1},{1,0},{2,3},{3,2},{4,5},{5,4},{6,7},{7,6},{8,9},{9,8},{10,11... | collective-permute-start | bytes 196616 | tf_op jit(solution)/shard_map/ppermute | solution.py:16
  300.6 5.8 %collective-permute-start.5 = (f32[64,256]{1,0:T(8,128)S(1)}, f32[64,256]{1,0:T(8,128)S(1)}, u32[]{:S(2)}, u32[]{:S(2)}) collective-permute-start(f32[64,256]{1,0:T(8,128)S(1)} %fusion.68), channel_id=1, source_target_pairs={{0,2},{1,3},{2,0},{3,1},{4,6},{5,7},{6,4},{7,5},{8,10},{9,11},{10,... | collective-permute-start | bytes 196616 | tf_op jit(solution)/shard_map/ppermute | solution.py:16
  303.8 6.1 %collective-permute-start.3 = (f32[64,256]{1,0:T(8,128)S(1)}, f32[64,256]{1,0:T(8,128)S(1)}, u32[]{:S(2)}, u32[]{:S(2)}) collective-permute-start(f32[64,256]{1,0:T(8,128)S(1)} %get-tuple-element.108), channel_id=1, source_target_pairs={{0,2},{1,3},{2,0},{3,1},{4,6},{5,7},{6,4},{7,5},{8,10},{9,11},{10,... | collective-permute-start | bytes 196616 | tf_op jit(solution)/shard_map/ppermute | solution.py:16
Sparse Core Ops, SparseCore 0:
  9.7 34.5 all-gather.2
  135.4 102.2 all-reduce.1
where the time goes:
time: 334 us
  waiting for transfers between devices  101 us (30%)
  matrix products  73.3 us (22%)
  other arithmetic  64.5 us (19%)
  blocking collectives  37.8 us (11%)
  between operations  16.6 us (5%)
  loops' own time  15.6 us (5%)
  local copies, waits for them, and re-layouts  15.3 us (5%)
  starting transfers between devices  9.94 us (3%)
    psum x1, waiting for transfers between devices, local(): summed = lax.psum(lax.map(one_block, starts).reshape(row_span, -1), 'col')  87.9 us
    dot_general x8, matrix products, one_block(): return jnp.dot(kernel_tile, probe_cols, preferred_element_type=jnp.float32)  66.3 us
    another operation x13, other arithmetic, interpolate(): jnp.linalg.cholesky(gram_mat + damping * jnp.eye(chosen.shape[0], dtype=s...  31.4 us
    another operation x9, other arithmetic, interpolate(): solved = jax.scipy.linalg.cho_solve((factor, True), cross_mat.T)  26.6 us
    all_gather x1, blocking collectives, local(): row_coords = lax.all_gather(points[:, 0], 'col', axis=1, tiled=True)  25.1 us
    another operation x1, loops' own time, local(): summed = lax.psum(lax.map(one_block, starts).reshape(row_span, -1), 'col')  15.6 us
    all_gather x1, blocking collectives, local(): lax.all_gather(points, 'row', axis=2, tiled=True)  12.7 us
    ppermute x6, waiting for transfers between devices, swapped(): lax.ppermute(value, axis, [(i, i ^ 1 << bit) for i in range(lax.axis_size...  12 us
  transfers between devices with their start and end apart: 8, of which 7 were waited for; matrix products, arithmetic and copies ran while one was open for 2% of the time, Pallas kernels for 0%

commit v1 on v0

--- a/solution.py
+++ b/solution.py
@@ -4,12 +4,259 @@
 import jax
 import jax.numpy as jnp
 from jax import lax
+from jax.experimental import pallas as pl
+from jax.experimental.pallas import tpu as pltpu
 from jax.sharding import PartitionSpec as P
 
 LEAF = 128
-
-
+MESH = pl.DeviceIdType.MESH
 exact_mode = lax.Precision.HIGHEST
+LOG2E = math.log2(math.e)
+SIDE = 4
+OWN = 256
+CHUNK = 4 * OWN
+FEATS = 64
+PLACE = {(0, 0): 0, (0, 1): 1, (1, 0): 2, (3, 0): 3, (1, 1): 4, (3, 1): 5, (2, 0): 6, (2, 1): 7}
+EARLY = 3
+
+
+def pieces(value):
+    high = value.astype(jnp.bfloat16).astype(jnp.float32)
+    rest = value - high
+    mid = rest.astype(jnp.bfloat16).astype(jnp.float32)
+    return high, mid, rest - mid
+
+
+def extra_rows(first, second):
+    row = lax.broadcasted_iota(jnp.int32, (16, OWN), 0)
+    out = jnp.zeros((16, OWN), jnp.float32)
+    for i, value in enumerate((*first, *second)):
+        out = jnp.where(row == i, value, out)
+    return out
+
+
+def spread(i):
+    return lax.rem(2 + i + lax.div(i * (i - 1), 2), SIDE)
+
+
+def sample_kernel(gain, probes, points, out, prb, pts, rpts, colf, rowf, acc, outbox, inbox,
+                  loc_sem, rp_send, rp_recv, chip_send, up_send, down_send, got, box_send, box_recv):
+    row, col = lax.axis_index("row"), lax.axis_index("col")
+    y, core = row // 2, lax.rem(row, 2)
+    x, z = col // SIDE, lax.rem(col, SIDE)
+    up = lax.rem(y + 1, SIDE) * 2 + core
+    down = lax.rem(y + 3, SIDE) * 2 + core
+    partner = y * 2 + 1 - core
+
+    local = [pltpu.make_async_copy(probes.at[q], prb.at[pl.ds(q * OWN, OWN)], loc_sem.at[q]) for q in range(4)]
+    local.append(pltpu.make_async_copy(points, pts.at[0], loc_sem.at[4]))
+    local.append(pltpu.make_async_copy(points.at[0], rpts.at[0], loc_sem.at[5]))
+    for copy in local:
+        copy.start()
+
+    def peer_col(j, sign):
+        dx, dz = j // SIDE, lax.rem(j, SIDE)
+        return lax.rem(x + sign * dx + SIDE, SIDE) * SIDE + lax.rem(z + sign * dz + SIDE, SIDE)
+
+    barrier = pltpu.get_barrier_semaphore()
+    for other in (up, down, partner):
+        pl.semaphore_signal(barrier, inc=1, device_id=(other, col), device_id_type=MESH)
+
+    def greet(j, _):
+        pl.semaphore_signal(barrier, inc=1, device_id=(row, peer_col(j, 1)), device_id_type=MESH)
+        return 0
+
+    lax.fori_loop(1, 16, greet, 0)
+    for copy in local:
+        copy.wait()
+    pl.semaphore_wait(barrier, 18)
+
+    def row_copy(j):
+        return pltpu.make_async_remote_copy(
+            src_ref=rpts.at[0], dst_ref=rpts.at[j], send_sem=rp_send.at[j], recv_sem=rp_recv.at[j],
+            device_id=(row, peer_col(j, 1)), device_id_type=MESH)
+
+    def send_row(j, _):
+        row_copy(j).start()
+        return 0
+
+    def piece_copy(src, dst, q, sem, target):
+        src_ref = pts.at[src] if q == 4 else prb.at[pl.ds(src * CHUNK + q * OWN, OWN)]
+        dst_ref = pts.at[dst] if q == 4 else prb.at[pl.ds(dst * CHUNK + q * OWN, OWN)]
+        return pltpu.make_async_remote_copy(
+            src_ref=src_ref, dst_ref=dst_ref, send_sem=sem, recv_sem=got.at[dst, q],
+            device_id=(target, col), device_id_type=MESH)
+
+    def on_chip(dy, q):
+        return piece_copy(PLACE[dy, 0], PLACE[dy, 1], q, chip_send.at[dy, q], partner)
+
+    def upward(src_dy, q):
+        return piece_copy(PLACE[src_dy, 0], PLACE[src_dy + 1, 0], q, up_send.at[src_dy, q], up)
+
+    def downward(src_dy, q):
+        return piece_copy(PLACE[src_dy, 0], PLACE[3 if src_dy == 0 else 2, 0], q, down_send.at[src_dy // 3, q], down)
+
+    def arrived(dy, dc, q):
+        place = PLACE[dy, dc]
+        piece_copy(place, place, q, chip_send.at[0, 0], partner).wait_recv()
+
+    on_chip(0, 4).start()
+    upward(0, 4).start()
+    downward(0, 4).start()
+    lax.fori_loop(1, 16, send_row, 0)
+    for q in range(4):
+        on_chip(0, q).start()
+    for q, r in zip((0, 1, 2, 3), (2, 3, 0, 1)):
+        upward(0, q).start()
+        downward(0, r).start()
+
+    def col_features(place):
+        for q in range(4):
+            feats = pts[place, q].astype(jnp.float32)
+            bias = jnp.sum(feats * feats, axis=0, keepdims=True) * (-LOG2E / 32)
+            ones = (jnp.float32(1),) * 3
+            stacked = jnp.concatenate([feats, feats, feats, extra_rows(ones, pieces(bias))], axis=0)
+            colf[:, pl.ds(place * CHUNK + q * OWN, OWN)] = stacked.astype(jnp.bfloat16)
+
+    def row_features(j):
+        feats = rpts[j].astype(jnp.float32)
+        bias = math.log2(gain) - jnp.sum(feats * feats, axis=0, keepdims=True) * (LOG2E / 32)
+        ones = (jnp.float32(1),) * 3
+        stacked = jnp.concatenate([*pieces(feats * (LOG2E / 16)), extra_rows(pieces(bias), ones)], axis=0)
+        rowf[pl.ds(pl.multiple_of(j * OWN, OWN), OWN), :] = stacked.T.astype(jnp.bfloat16)
+
+    def block(j, first, last):
+        rows = rowf[pl.ds(pl.multiple_of(j * OWN, OWN), OWN), :]
+        cols = pl.ds(first * CHUNK, (last - first) * CHUNK)
+        power = jnp.dot(rows, colf[:, cols], preferred_element_type=jnp.float32)
+        return jnp.exp2(power).astype(jnp.bfloat16), prb[cols, :]
+
+    def at(j):
+        return pl.ds(pl.multiple_of(j * OWN, OWN), OWN)
+
+    col_features(0)
+    row_features(0)
+    power = jnp.dot(rowf[pl.ds(0, OWN), :], colf[:, pl.ds(0, CHUNK)], preferred_element_type=jnp.float32)
+    leaf_of = lax.broadcasted_iota(jnp.int32, (OWN, CHUNK), 0) // LEAF
+    other_leaf = lax.broadcasted_iota(jnp.int32, (OWN, CHUNK), 1) // LEAF
+    tile = jnp.where(leaf_of == other_leaf, 0.0, jnp.exp2(power)).astype(jnp.bfloat16)
+    own_sum = jnp.dot(tile, prb[pl.ds(0, CHUNK), :], preferred_element_type=jnp.float32)
+    for q in (4, 0, 1, 2, 3):
+        arrived(0, 1, q)
+    col_features(1)
+    tile, rows = block(0, 1, 2)
+    acc[pl.ds(0, OWN), :] = own_sum + jnp.dot(tile, rows, preferred_element_type=jnp.float32)
+
+    def near_block(j, _):
+        row_copy(j).wait_recv()
+        row_features(j)
+        tile, rows = block(j, 0, 2)
+        acc[at(j), :] = jnp.dot(tile, rows, preferred_element_type=jnp.float32)
+
+        @pl.when(j == 10)
+        def _():
+            for q in (4, 0, 1):
+                arrived(1, 0, q)
+                upward(1, q).start()
+                on_chip(1, q).start()
+            for q in (4, 2, 3):
+                arrived(3, 0, q)
+                if q != 4:
+                    downward(3, q).start()
+                on_chip(3, q).start()
+        return 0
+
+    lax.fori_loop(1, 16, near_block, 0)
+    for q, r in ((2, 0), (3, 1)):
+        arrived(1, 0, q)
+        on_chip(1, q).start()
+        arrived(3, 0, r)
+        on_chip(3, r).start()
+    for place in range(2, EARLY):
+        col_features(place)
+
+    def mid_block(j, _):
+        tile, rows = block(j, 2, EARLY)
+        acc[at(j), :] += jnp.dot(tile, rows, preferred_element_type=jnp.float32)
+
+        @pl.when(j == 12)
+        def _():
+            for q in (4, 0, 2, 1, 3):
+                arrived(2, 0, q)
+                on_chip(2, q).start()
+        return 0
+
+    lax.fori_loop(0, 16, mid_block, 0)
+    for dy in (1, 3, 2):
+        for q in (4, 0, 1, 2, 3):
+            arrived(dy, 1, q)
+    for place in range(EARLY, 8):
+        col_features(place)
+
+    def box_copy(j):
+        return pltpu.make_async_remote_copy(
+            src_ref=outbox.at[j], dst_ref=inbox.at[j], send_sem=box_send.at[j], recv_sem=box_recv.at[j],
+            device_id=(row, peer_col(j, -1)), device_id_type=MESH)
+
+    def last_block(i, _):
+        j = spread(i // SIDE) * SIDE + spread(lax.rem(i, SIDE))
+        tile, rows = block(j, EARLY, 8)
+        total = acc[at(j), :] + jnp.dot(tile, rows, preferred_element_type=jnp.float32)
+        outbox[j] = total.astype(jnp.bfloat16)
+        box_copy(j).start()
+        return 0
+
+    lax.fori_loop(0, 15, last_block, 0)
+    tile, rows = block(0, EARLY, 8)
+    acc[pl.ds(0, OWN), :] += jnp.dot(tile, rows, preferred_element_type=jnp.float32)
+
+    def take(i, _):
+        j = spread(i // SIDE) * SIDE + spread(lax.rem(i, SIDE))
+        box_copy(j).wait_recv()
+        acc[pl.ds(0, OWN), :] += inbox[j].astype(jnp.float32)
+        return 0
+
+    lax.fori_loop(0, 15, take, 0)
+    out[...] = acc[pl.ds(0, OWN), :]
+
+    def drain(j, _):
+        row_copy(j).wait_send()
+        box_copy(j).wait_send()
+        return 0
+
+    lax.fori_loop(1, 16, drain, 0)
+    for q in range(5):
+        for dy in range(4):
+            on_chip(dy, q).wait_send()
+        upward(0, q).wait_send()
+        downward(0, q).wait_send()
+    for q in (4, 0, 1):
+        upward(1, q).wait_send()
+    for q in (2, 3):
+        downward(3, q).wait_send()
+
+
+def sample_rows(probes, points, gain):
+    bf16, f32, dma = jnp.bfloat16, jnp.float32, pltpu.SemaphoreType.DMA
+    rows = 16 * OWN
+    return pl.pallas_call(
+        partial(sample_kernel, gain),
+        out_shape=jax.ShapeDtypeStruct((OWN, 256), f32),
+        in_specs=[pl.BlockSpec(memory_space=pl.ANY), pl.BlockSpec(memory_space=pl.ANY)],
+        out_specs=pl.BlockSpec(memory_space=pltpu.VMEM),
+        scratch_shapes=[
+            pltpu.VMEM((8 * CHUNK, 256), bf16),
+            pltpu.VMEM((8, 4, 16, OWN), bf16),
+            pltpu.VMEM((16, 16, OWN), bf16),
+            pltpu.VMEM((FEATS, 8 * CHUNK), bf16),
+            pltpu.VMEM((rows, FEATS), bf16),
+            pltpu.VMEM((rows, 256), f32),
+            pltpu.VMEM((16, OWN, 256), bf16),
+            pltpu.VMEM((16, OWN, 256), bf16),
+            dma((6,)), dma((16,)), dma((16,)), dma((4, 5)), dma((2, 5)), dma((2, 5)), dma((8, 5)), dma((16,)), dma((16,)),
+        ],
+        compiler_params=pltpu.CompilerParams(collective_id=0, has_side_effects=True, vmem_limit_bytes=60 << 20),
+    )(probes, points)
 
 
 def swapped(value, axis, bit):
@@ -72,51 +319,10 @@
 def local(probes, points, leaf_skeleton, skeleton_one, skeleton_two, skeleton_three):
     feat_count = points.shape[0]
     own_rows = probes.shape[1]
-    row_count = lax.axis_size("row")
-    col_count = lax.axis_size("col")
-    row_pos = lax.axis_index("row")
     col_pos = lax.axis_index("col")
-    row_span = own_rows * col_count
-    extent = row_span * row_count
+    extent = own_rows * lax.axis_size("row") * lax.axis_size("col")
     kernel_gain = 16.0 / math.sqrt(4 * extent)
-    probe_cols = lax.all_gather(probes, "row", axis=1, tiled=True).reshape(
-        4 * row_count * own_rows, -1
-    )
-    row_coords = lax.all_gather(points[:, 0], "col", axis=1, tiled=True)
-    col_coords = lax.all_gather(points, "row", axis=2, tiled=True).reshape(
-        feat_count, 4 * row_count * own_rows
-    )
-    col_wide = col_coords.astype(jnp.float32)
-    col_sq = jnp.sum(col_wide * col_wide, axis=0)
-    row_leaf = (row_pos * row_span + jnp.arange(row_span, dtype=jnp.int32)) // LEAF
-    quarter_len = row_count * own_rows
-    offsets = jnp.arange(4 * quarter_len, dtype=jnp.int32)
-    quarter = offsets // quarter_len
-    within = offsets % quarter_len
-    col_leaf = (
-        quarter * extent + within // own_rows * row_span + col_pos * own_rows + within % own_rows
-    ) // LEAF
-    height = 512
-
-    def one_block(first_row):
-        coords = lax.dynamic_slice_in_dim(row_coords, first_row, height, 1)
-        leaves = lax.dynamic_slice_in_dim(row_leaf, first_row, height, 0)
-        cross = lax.dot_general(
-            coords, col_coords, (((0,), (0,)), ((), ())), preferred_element_type=jnp.float32
-        )
-        row_wide = coords.astype(jnp.float32)
-        row_sq = jnp.sum(row_wide * row_wide, axis=0)
-        kernel_tile = kernel_gain * jnp.exp(
-            (2.0 * cross - row_sq[:, None] - col_sq[None, :]) / (2.0 * feat_count)
-        )
-        kernel_tile = jnp.where(leaves[:, None] == col_leaf[None, :], 0.0, kernel_tile).astype(
-            jnp.bfloat16
-        )
-        return jnp.dot(kernel_tile, probe_cols, preferred_element_type=jnp.float32)
-
-    starts = jnp.arange(row_span // height, dtype=jnp.int32) * height
-    summed = lax.psum(lax.map(one_block, starts).reshape(row_span, -1), "col")
-    owned = lax.dynamic_slice_in_dim(summed, col_pos * own_rows, own_rows, 0)
+    owned = sample_rows(probes, points.transpose(1, 0, 2), kernel_gain)
     leaf_count = own_rows // LEAF
     leaf_rows = owned.reshape(leaf_count, LEAF, -1)
     leaf_probes = probes[0].reshape(leaf_count, LEAF, -1)

time: 334 us -> 174 us (0.52)
  waiting for transfers between devices: 101 us -> 7.03 us
  Pallas kernels: 0 us -> 71.7 us
  matrix products: 73.3 us -> 7.05 us
  blocking collectives: 37.8 us -> 0 us
  loops' own time: 15.6 us -> 0 us
  between operations: 16.6 us -> 3.18 us
  local copies, waits for them, and re-layouts: 15.3 us -> 11.1 us
    psum x1 -> x0, waiting for transfers between devices: 87.9 us -> none  [local(): summed = lax.psum(lax.map(one_block, starts).reshape(row_span, -1), 'col')]
    pallas_call x0 -> x1, Pallas kernels: none -> 71.7 us  [sample_rows(): pl.pallas_call(partial(sample_kernel, gain), out_shape=jax.ShapeDtypeStru...]
    dot_general x8 -> x0, matrix products: 66.3 us -> none  [one_block(): return jnp.dot(kernel_tile, probe_cols, preferred_element_type=jnp.float32)]
    all_gather x2 -> x0, blocking collectives: 37.8 us -> none  [the longest x1 25.1 us: local(): row_coords = lax.all_gather(points[:, 0], 'col', axis=1, tiled=True)]
    another operation x1 -> x0, loops' own time: 15.6 us -> none  [local(): summed = lax.psum(lax.map(one_block, starts).reshape(row_span, -1), 'col')]
    dynamic_slice x17 -> x0, local copies, waits for them, and re-layouts: 6.28 us -> none  [the longest x8 4.66 us: local(): summed = lax.psum(lax.map(one_block, starts).reshape(row_span, -1), 'col')]
    ppermute x6, waiting for transfers between devices: 12 us -> 7.03 us  [swapped(): lax.ppermute(value, axis, [(i, i ^ 1 << bit) for i in range(lax.axis_size...]
  transfers between devices with their start and end apart: 8 -> 6, of which waited for: 7 -> 3; matrix products, arithmetic and copies ran while one was open for 2% -> 10% of each run, Pallas kernels for 0% -> 0%
where the time goes in v1:
time: 174 us
  Pallas kernels  71.7 us (41%)
  other arithmetic  63.9 us (37%)
  local copies, waits for them, and re-layouts  11.1 us (6%)
  starting transfers between devices  10 us (6%)
  matrix products  7.05 us (4%)
  waiting for transfers between devices  7.03 us (4%)
  between operations  3.18 us (2%)
    pallas_call x1, Pallas kernels, sample_rows(): pl.pallas_call(partial(sample_kernel, gain), out_shape=jax.ShapeDtypeStru...  71.7 us
    another operation x13, other arithmetic, interpolate(): jnp.linalg.cholesky(gram_mat + damping * jnp.eye(chosen.shape[0], dtype=s...  31.4 us
    another operation x9, other arithmetic, interpolate(): solved = jax.scipy.linalg.cho_solve((factor, True), cross_mat.T)  26.6 us
    ppermute x6, starting transfers between devices, swapped(): lax.ppermute(value, axis, [(i, i ^ 1 << bit) for i in range(lax.axis_size...  10 us
    ppermute x6, waiting for transfers between devices, swapped(): lax.ppermute(value, axis, [(i, i ^ 1 << bit) for i in range(lax.axis_size...  7.03 us
    gather x5, local copies, waits for them, and re-layouts, interpolate(): skeleton = jnp.take(stacked, chosen, axis=0)  3.96 us
  transfers between devices with their start and end apart: 6, of which 3 were waited for; matrix products, arithmetic and copies ran while one was open for 10% of the time, Pallas kernels for 0%

profile of v1, /device:TPU:0, one launch (start us, length us, event | category | flops | bytes accessed | tf_op | source)
XLA Modules:
  0.0 174.0 jit_solution(2983083554632344211)
XLA Ops:
  0.6 0.8 bitcast_or_fusion
  1.4 1.4 copy.61
  2.9 71.7 %shard_map.85 = f32[256,256]{1,0:T(8,128)} custom-call(bf16[4,256,256]{2,1,0:T(8,128)(2,1)} %probes.1, bf16[4,16,256]{2,1,0:T(8,128)(2,1)} %bitcast.183), custom_call_target="tpu_custom_call" | custom-call | tf_op jit(solution)/shard_map/pallas_call | solution.py:242
  74.6 1.9 %gather_fusion = f32[128,256]{1,0:T(8,128)S(1)} fusion(f32[2,128,256]{2,1,0:T(8,128)} %bitcast.174, s32[128]{0:T(128)S(1)} %reshape.113), kind=kCustom, calls=%fused_computation.5 | custom fusion | bytes 263168 | tf_op jit(solution)/shard_map/vmap(jit(_take))/gather | solution.py:277
  76.7 0.8 copy-done
  78.2 0.7 copy-done.2
  79.0 1.1 gather_fusion.1
  81.4 11.7 %custom-call.18 = f32[2,64,64]{2,1,0:T(8,128)S(1)} custom-call(f32[2,64,64]{2,1,0:T(8,128)S(1)} %fusion.46), custom_call_target="Cholesky" | custom-call | tf_op jit(solution)/shard_map/vmap(jit(cholesky))/cholesky | solution.py:280
  93.5 9.8 %custom-call.19 = f32[2,1,64,64]{2,3,1,0:T(8,128)S(1)} custom-call(f32[2,1,64,64]{3,2,1,0:T(8,128)S(1)} %select_bitcast_fusion), custom_call_target="InvertDiagBlocksLowerTriangular" | custom-call | tf_op jit(solution)/shard_map/vmap(jit(_cho_solve))/triangular_solve | solution.py:282
  103.9 0.7 slice-done
  105.2 0.7 gather_fusion.2
  105.9 0.7 multiply_reduce_fusion.3
  107.4 2.3 %collective-permute-start.1 = (f32[16,64]{0,1:T(8,128)S(1)}, f32[16,64]{0,1:T(8,128)S(1)}, u32[]{:S(2)}, u32[]{:S(2)}) collective-permute-start(f32[16,64]{0,1:T(8,128)S(1)} %select_bitcast_fusion.3), channel_id=1, source_target_pairs={{0,1},{1,0},{2,3},{3,2},{4,5},{5,4},{6,7},{7,6},{8,9},{9,8},{10,11... | collective-permute-start | bytes 12296 | tf_op jit(solution)/shard_map/ppermute | solution.py:263
  110.9 5.8 %cholesky.106 = f32[64,64]{1,0:T(8,128)S(1)} custom-call(f32[64,64]{1,0:T(8,128)S(1)} %fusion.67), custom_call_target="Cholesky" | custom-call | tf_op jit(solution)/shard_map/jit(cholesky)/cholesky | solution.py:280
  117.4 0.7 fusion.50
  118.1 4.9 %custom-call.26 = f32[1,64,64]{1,2,0:T(8,128)S(1)} custom-call(f32[1,64,64]{2,1,0:T(8,128)S(1)} %fusion.50), custom_call_target="InvertDiagBlocksLowerTriangular" | custom-call | tf_op jit(solution)/shard_map/jit(_cho_solve)/triangular_solve | solution.py:282
  123.7 0.7 compare_and_fusion
  125.4 4.0 %collective-permute-start.4 = (f32[16,64]{0,1:T(8,128)S(1)}, f32[16,64]{0,1:T(8,128)S(1)}, u32[]{:S(2)}, u32[]{:S(2)}) collective-permute-start(f32[16,64]{0,1:T(8,128)S(1)} %select_bitcast_fusion.2), channel_id=1, source_target_pairs={{0,2},{1,3},{2,0},{3,1},{4,6},{5,7},{6,4},{7,5},{8,10},{9,11},{10,... | collective-permute-start | bytes 12296 | tf_op jit(solution)/shard_map/ppermute | solution.py:263
  129.8 1.5 collective-permute-done.4
  132.1 0.7 gather_fusion.4
  132.8 0.7 multiply_reduce_fusion.2
  134.7 5.8 %cholesky.117 = f32[64,64]{1,0:T(8,128)S(1)} custom-call(f32[64,64]{1,0:T(8,128)S(1)} %fusion.62), custom_call_target="Cholesky" | custom-call | tf_op jit(solution)/shard_map/jit(cholesky)/cholesky | solution.py:280
  141.9 4.9 %custom-call.27 = f32[1,64,64]{1,2,0:T(8,128)S(1)} custom-call(f32[1,64,64]{2,1,0:T(8,128)S(1)} %fusion.51), custom_call_target="InvertDiagBlocksLowerTriangular" | custom-call | tf_op jit(solution)/shard_map/jit(_cho_solve)/triangular_solve | solution.py:282
  147.4 3.6 %collective-permute-start.5 = (f32[64,256]{1,0:T(8,128)S(1)}, f32[64,256]{1,0:T(8,128)S(1)}, u32[]{:S(2)}, u32[]{:S(2)}) collective-permute-start(f32[64,256]{1,0:T(8,128)S(1)} %fusion.34), channel_id=1, source_target_pairs={{0,2},{1,3},{2,0},{3,1},{4,6},{5,7},{6,4},{7,5},{8,10},{9,11},{10,... | collective-permute-start | bytes 196616 | tf_op jit(solution)/shard_map/ppermute | solution.py:263
  151.3 2.0 %collective-permute-done.5 = f32[64,256]{1,0:T(8,128)S(1)} collective-permute-done((f32[64,256]{1,0:T(8,128)S(1)}, f32[64,256]{1,0:T(8,128)S(1)}, u32[]{:S(2)}, u32[]{:S(2)}) %collective-permute-start.5) | collective-permute-done | bytes 65568 | tf_op jit(solution)/shard_map/ppermute | solution.py:263
  153.5 3.5 %collective-permute-done.3 = f32[64,256]{1,0:T(8,128)S(1)} collective-permute-done((f32[64,256]{1,0:T(8,128)S(1)}, f32[64,256]{1,0:T(8,128)S(1)}, u32[]{:S(2)}, u32[]{:S(2)}) %collective-permute-start.3) | collective-permute-done | bytes 65568 | tf_op jit(solution)/shard_map/ppermute | solution.py:263
  157.3 0.7 gather_fusion.6
  158.2 0.7 select_bitcast_fusion.1
  159.9 5.8 %cholesky.128 = f32[64,64]{1,0:T(8,128)S(1)} custom-call(f32[64,64]{1,0:T(8,128)S(1)} %fusion.57), custom_call_target="Cholesky" | custom-call | tf_op jit(solution)/shard_map/jit(cholesky)/cholesky | solution.py:280
  166.5 0.7 fusion.52
  167.1 4.9 %custom-call.28 = f32[1,64,64]{1,2,0:T(8,128)S(1)} custom-call(f32[1,64,64]{2,1,0:T(8,128)S(1)} %fusion.52), custom_call_target="InvertDiagBlocksLowerTriangular" | custom-call | tf_op jit(solution)/shard_map/jit(_cho_solve)/triangular_solve | solution.py:282
  172.7 0.7 maximum_bitcast_fusion
  (102 shorter events, 14.4 us)
Async XLA Ops:
  0.6 0.8 copy-start.3
  76.5 1.0 copy-start
  78.1 0.8 copy-start.2
  80.5 0.7 copy-start.4
  103.6 0.9 slice-start
  103.8 0.9 copy-start.1
  106.5 25.3 %collective-permute-start = (f32[64,256]{1,0:T(8,128)S(1)}, f32[64,256]{1,0:T(8,128)S(1)}, u32[]{:S(2)}, u32[]{:S(2)}) collective-permute-start(f32[64,256]{1,0:T(8,128)S(1)} %get-tuple-element.23), channel_id=1, source_target_pairs={{0,1},{1,0},{2,3},{3,2},{4,5},{5,4},{6,7},{7,6},{8,9},{9,8},{10,11... | collective-permute-start | bytes 196616 | tf_op jit(solution)/shard_map/ppermute | solution.py:263
  107.4 17.1 %collective-permute-start.1 = (f32[16,64]{0,1:T(8,128)S(1)}, f32[16,64]{0,1:T(8,128)S(1)}, u32[]{:S(2)}, u32[]{:S(2)}) collective-permute-start(f32[16,64]{0,1:T(8,128)S(1)} %select_bitcast_fusion.3), channel_id=1, source_target_pairs={{0,1},{1,0},{2,3},{3,2},{4,5},{5,4},{6,7},{7,6},{8,9},{9,8},{10,11... | collective-permute-start | bytes 12296 | tf_op jit(solution)/shard_map/ppermute | solution.py:263
  123.6 8.0 %collective-permute-start.2 = (f32[64,256]{1,0:T(8,128)S(1)}, f32[64,256]{1,0:T(8,128)S(1)}, u32[]{:S(2)}, u32[]{:S(2)}) collective-permute-start(f32[64,256]{1,0:T(8,128)S(1)} %fusion.30), channel_id=1, source_target_pairs={{0,1},{1,0},{2,3},{3,2},{4,5},{5,4},{6,7},{7,6},{8,9},{9,8},{10,11... | collective-permute-start | bytes 196616 | tf_op jit(solution)/shard_map/ppermute | solution.py:263
  125.4 5.9 %collective-permute-start.4 = (f32[16,64]{0,1:T(8,128)S(1)}, f32[16,64]{0,1:T(8,128)S(1)}, u32[]{:S(2)}, u32[]{:S(2)}) collective-permute-start(f32[16,64]{0,1:T(8,128)S(1)} %select_bitcast_fusion.2), channel_id=1, source_target_pairs={{0,2},{1,3},{2,0},{3,1},{4,6},{5,7},{6,4},{7,5},{8,10},{9,11},{10,... | collective-permute-start | bytes 12296 | tf_op jit(solution)/shard_map/ppermute | solution.py:263
  147.4 5.9 %collective-permute-start.5 = (f32[64,256]{1,0:T(8,128)S(1)}, f32[64,256]{1,0:T(8,128)S(1)}, u32[]{:S(2)}, u32[]{:S(2)}) collective-permute-start(f32[64,256]{1,0:T(8,128)S(1)} %fusion.34), channel_id=1, source_target_pairs={{0,2},{1,3},{2,0},{3,1},{4,6},{5,7},{6,4},{7,5},{8,10},{9,11},{10,... | collective-permute-start | bytes 196616 | tf_op jit(solution)/shard_map/ppermute | solution.py:263
  151.2 5.8 %collective-permute-start.3 = (f32[64,256]{1,0:T(8,128)S(1)}, f32[64,256]{1,0:T(8,128)S(1)}, u32[]{:S(2)}, u32[]{:S(2)}) collective-permute-start(f32[64,256]{1,0:T(8,128)S(1)} %get-tuple-element.21), channel_id=1, source_target_pairs={{0,2},{1,3},{2,0},{3,1},{4,6},{5,7},{6,4},{7,5},{8,10},{9,11},{10,... | collective-permute-start | bytes 196616 | tf_op jit(solution)/shard_map/ppermute | solution.py:263

commit v2 on v1

--- a/solution.py
+++ b/solution.py
@@ -27,20 +27,93 @@
     return high, mid, rest - mid
 
 
-def extra_rows(first, second):
-    row = lax.broadcasted_iota(jnp.int32, (16, OWN), 0)
-    out = jnp.zeros((16, OWN), jnp.float32)
+def extra_rows(first, second, width=OWN):
+    row = lax.broadcasted_iota(jnp.int32, (16, width), 0)
+    out = jnp.zeros((16, width), jnp.float32)
     for i, value in enumerate((*first, *second)):
         out = jnp.where(row == i, value, out)
     return out
 
 
+def exact(a, b, dims=((1,), (0,))):
+    return lax.dot_general(a, b, (dims, ((), ())), precision=exact_mode, preferred_element_type=jnp.float32)
+
+def split(v):
+    h = v.astype(jnp.bfloat16)
+    r = v - h.astype(jnp.float32)
+    m = r.astype(jnp.bfloat16)
+    return h, m, (r - m.astype(jnp.float32)).astype(jnp.bfloat16)
+
+def select_rows(pick, values):
+    return jnp.dot(jnp.concatenate([pick] * 3, axis=1), jnp.concatenate(split(values), axis=0), preferred_element_type=jnp.float32)
+
+def pick_of(chosen):
+    hits = lax.broadcasted_iota(jnp.int32, (128, 64), 0) == chosen
+    return hits.astype(jnp.float32).T.astype(jnp.bfloat16)
+
+def wide(col, width):
+    return jnp.concatenate([col, col[:, :width - 128]], axis=1) if width > 128 else col[:, :width]
+
+def eliminate(systems):
+    width = systems[0].shape[1]
+    sub = lax.broadcasted_iota(jnp.int32, (8, 1), 0)
+    systems = [[m[8 * i:8 * i + 8, :] for i in range(8)] for m in systems]
+    for b in range(8):
+        for m in systems:
+            cols = [[jnp.broadcast_to(m[i][:, 8 * b + j:8 * b + j + 1], (8, 128)) for j in range(8)] for i in range(8)]
+            p, lead = m[b], list(cols[b])
+            for k in range(8):
+                inv = 1.0 / lead[k][k:k + 1, :]
+                f = lead[k] * inv
+                q = p[k:k + 1, :]
+                p = jnp.where(sub == k, q * wide(inv, width), p - wide(f, width) * q)
+                for j in range(k + 1, 8):
+                    q = lead[j][k:k + 1, :]
+                    lead[j] = jnp.where(sub == k, q * inv, lead[j] - f * q)
+            m[b] = p
+            for i in range(8):
+                if i != b:
+                    total = m[i]
+                    for k in range(8):
+                        total = total - wide(cols[i][k], width) * p[k:k + 1, :]
+                    m[i] = total
+    return [jnp.concatenate(m, axis=0)[:, 64:] for m in systems]
+
+def interpolate(stacked, picks, keep=None):
+    systems, kept = [], []
+    eye = lax.broadcasted_iota(jnp.int32, (64, 64), 0) == lax.broadcasted_iota(jnp.int32, (64, 64), 1)
+    for y, pick in zip(stacked, picks):
+        z = select_rows(pick, y)
+        kept.append(z)
+        if keep is not None:
+            keep(z)
+        cross = exact(z, y, ((1,), (1,)))
+        gram = lax.dot_general(jnp.concatenate(split(cross), axis=1), jnp.concatenate([pick] * 3, axis=1), (((1,), (1,)), ((), ())), preferred_element_type=jnp.float32)
+        diag = jnp.where(eye, gram, 0.0)
+        ridge = jnp.sum(diag, keepdims=True) * (0.05 / 64) + 1e-5
+        gram = gram + jnp.where(eye, ridge, 0.0)
+        systems.append(jnp.concatenate([gram, cross], axis=1))
+    return eliminate(systems), kept
+
+
+def kernel_square(gain, feats):
+    sq = jnp.sum(feats * feats, axis=0, keepdims=True)
+    ones = (jnp.ones((1, 128), jnp.float32),) * 3
+    left = jnp.concatenate([*pieces(feats * (LOG2E / 16)), extra_rows(pieces(math.log2(gain) - sq * (LOG2E / 32)), ones, 128)], axis=0)
+    right = jnp.concatenate([feats, feats, feats, extra_rows(ones, pieces(sq * (-LOG2E / 32)), 128)], axis=0)
+    power = jnp.dot(left.T.astype(jnp.bfloat16), right.astype(jnp.bfloat16), preferred_element_type=jnp.float32)
+    child = lax.broadcasted_iota(jnp.int32, (128, 128), 0) // 64
+    other = lax.broadcasted_iota(jnp.int32, (128, 128), 1) // 64
+    return jnp.where(child == other, 0.0, jnp.exp2(power))
+
+
 def spread(i):
     return lax.rem(2 + i + lax.div(i * (i - 1), 2), SIDE)
 
 
-def sample_kernel(gain, probes, points, out, prb, pts, rpts, colf, rowf, acc, outbox, inbox,
-                  loc_sem, rp_send, rp_recv, chip_send, up_send, down_send, got, box_send, box_recv):
+def hss_kernel(gain, probes, points, chosen_leaf, chosen_one, chosen_two, chosen_three, leaf_out, upper_out, top_out,
+               prb, pts, rpts, colf, rowf, acc, outbox, inbox, picks, square, pair_p, pair_z, pair_r, leaf_x, upper_x, top_x,
+               loc_sem, rp_send, rp_recv, chip_send, up_send, down_send, got, box_send, box_recv, pair_send, pair_recv, out_sem):
     row, col = lax.axis_index("row"), lax.axis_index("col")
     y, core = row // 2, lax.rem(row, 2)
     x, z = col // SIDE, lax.rem(col, SIDE)
@@ -69,6 +142,35 @@
     lax.fori_loop(1, 16, greet, 0)
     for copy in local:
         copy.wait()
+
+    bits = (lax.rem(col, 2), lax.rem(col // 2, 2))
+
+    def pair_copy(level, kind):
+        bit = bits[level]
+        ref = pair_p.at[level, bit] if kind == 0 else (pair_z, pair_r)[kind - 1].at[level, pl.ds(pl.multiple_of(bit * 64, 64), 64)]
+        return pltpu.make_async_remote_copy(
+            src_ref=ref, dst_ref=ref, send_sem=pair_send.at[level, kind], recv_sem=pair_recv.at[level, kind],
+            device_id=(row, col + (1 - 2 * bit) * (level + 1)), device_id_type=MESH)
+
+    for leaf in range(2):
+        picks[leaf] = pick_of(chosen_leaf[leaf:leaf + 1, :])
+    picks[2] = pick_of(chosen_one[...])
+    picks[3] = pick_of(chosen_two[pl.ds(col // 2, 1), :])
+    picks[4] = pick_of(chosen_three[pl.ds(col // 4, 1), :])
+
+    def picked(feats, pick):
+        return lax.dot_general(feats, pick, (((1,), (1,)), ((), ())), preferred_element_type=jnp.float32)
+
+    def child_points(level, feats):
+        square[level] = kernel_square(gain, feats)
+        if level < 2:
+            pair_p[level, bits[level]] = picked(feats.astype(jnp.bfloat16), picks[2 + level]).astype(jnp.bfloat16)
+
+    def pair_points(level):
+        pair_copy(level, 0).wait_recv()
+        return jnp.concatenate([pair_p[level, 0], pair_p[level, 1]], axis=1).astype(jnp.float32)
+
+    child_points(0, jnp.concatenate([picked(pts[0, 0, :, leaf * LEAF:(leaf + 1) * LEAF], picks[leaf]) for leaf in range(2)], axis=1))
     pl.semaphore_wait(barrier, 18)
 
     def row_copy(j):
@@ -104,6 +206,7 @@
     upward(0, 4).start()
     downward(0, 4).start()
     lax.fori_loop(1, 16, send_row, 0)
+    pair_copy(0, 0).start()
     for q in range(4):
         on_chip(0, q).start()
     for q, r in zip((0, 1, 2, 3), (2, 3, 0, 1)):
@@ -174,6 +277,8 @@
         on_chip(3, r).start()
     for place in range(2, EARLY):
         col_features(place)
+    child_points(1, pair_points(0))
+    pair_copy(1, 0).start()
 
     def mid_block(j, _):
         tile, rows = block(j, 2, EARLY)
@@ -187,6 +292,7 @@
         return 0
 
     lax.fori_loop(0, 16, mid_block, 0)
+    child_points(2, pair_points(1))
     for dy in (1, 3, 2):
         for q in (4, 0, 1, 2, 3):
             arrived(dy, 1, q)
@@ -217,7 +323,41 @@
         return 0
 
     lax.fori_loop(0, 15, take, 0)
-    out[...] = acc[pl.ds(0, OWN), :]
+
+    def leave(src, dst, sem):
+        pltpu.make_async_copy(src, dst, sem).start()
+
+    solved, kept = interpolate([acc[pl.ds(leaf * LEAF, LEAF), :] for leaf in range(2)], [picks[0], picks[1]])
+    reduced = []
+    for leaf, value in enumerate(solved):
+        rows = prb[pl.ds(leaf * LEAF, LEAF), :]
+        reduced.append(jnp.dot(jnp.concatenate(split(value), axis=1), jnp.concatenate([rows] * 3, axis=0), preferred_element_type=jnp.float32))
+        leaf_x[leaf] = value.T
+    leave(leaf_x, leaf_out, out_sem.at[0])
+    below, weights = jnp.concatenate(kept, axis=0), jnp.concatenate(reduced, axis=0)
+    for level in range(3):
+        if level > 0:
+            pair_copy(level - 1, 1).wait_recv()
+            pair_copy(level - 1, 2).wait_recv()
+            below, weights = pair_z[level - 1], pair_r[level - 1]
+
+        def keep(value):
+            if level == 2:
+                top_x[0] = value
+            else:
+                pair_z[level, pl.ds(pl.multiple_of(bits[level] * 64, 64), 64), :] = value
+                pair_copy(level, 1).start()
+
+        solved, _ = interpolate([below - exact(square[level], weights)], [picks[2 + level]], keep)
+        value = exact(solved[0], weights)
+        if level == 2:
+            top_x[1] = value
+            leave(top_x, top_out, out_sem.at[4])
+        else:
+            pair_r[level, pl.ds(pl.multiple_of(bits[level] * 64, 64), 64), :] = value
+            pair_copy(level, 2).start()
+        upper_x[level] = solved[0].T
+        leave(upper_x.at[level], upper_out.at[level], out_sem.at[1 + level])
 
     def drain(j, _):
         row_copy(j).wait_send()
@@ -234,116 +374,53 @@
         upward(1, q).wait_send()
     for q in (2, 3):
         downward(3, q).wait_send()
-
-
-def sample_rows(probes, points, gain):
-    bf16, f32, dma = jnp.bfloat16, jnp.float32, pltpu.SemaphoreType.DMA
+    for level in range(2):
+        for kind in range(3):
+            pair_copy(level, kind).wait_send()
+    pltpu.make_async_copy(leaf_x, leaf_out, out_sem.at[0]).wait()
+    for level in range(3):
+        pltpu.make_async_copy(upper_x.at[level], upper_out.at[level], out_sem.at[1 + level]).wait()
+    pltpu.make_async_copy(top_x, top_out, out_sem.at[4]).wait()
+
+
+def local(probes, points, leaf_skeleton, skeleton_one, skeleton_two, skeleton_three):
+    bf16, f32, dma, vmem = jnp.bfloat16, jnp.float32, pltpu.SemaphoreType.DMA, pltpu.VMEM
+    extent = OWN * lax.axis_size("row") * lax.axis_size("col")
+    kernel_gain = 16.0 / math.sqrt(4 * extent)
     rows = 16 * OWN
-    return pl.pallas_call(
-        partial(sample_kernel, gain),
-        out_shape=jax.ShapeDtypeStruct((OWN, 256), f32),
-        in_specs=[pl.BlockSpec(memory_space=pl.ANY), pl.BlockSpec(memory_space=pl.ANY)],
-        out_specs=pl.BlockSpec(memory_space=pltpu.VMEM),
+    outside, inside = pl.BlockSpec(memory_space=pl.ANY), pl.BlockSpec(memory_space=vmem)
+    leaf_interp, upper_interp, top_state = pl.pallas_call(
+        partial(hss_kernel, kernel_gain),
+        out_shape=(
+            jax.ShapeDtypeStruct((2, LEAF, 64), f32),
+            jax.ShapeDtypeStruct((3, LEAF, 64), f32),
+            jax.ShapeDtypeStruct((2, 64, 256), f32),
+        ),
+        in_specs=[outside, outside, inside, inside, inside, inside],
+        out_specs=(outside, outside, outside),
         scratch_shapes=[
-            pltpu.VMEM((8 * CHUNK, 256), bf16),
-            pltpu.VMEM((8, 4, 16, OWN), bf16),
-            pltpu.VMEM((16, 16, OWN), bf16),
-            pltpu.VMEM((FEATS, 8 * CHUNK), bf16),
-            pltpu.VMEM((rows, FEATS), bf16),
-            pltpu.VMEM((rows, 256), f32),
-            pltpu.VMEM((16, OWN, 256), bf16),
-            pltpu.VMEM((16, OWN, 256), bf16),
+            vmem((8 * CHUNK, 256), bf16),
+            vmem((8, 4, 16, OWN), bf16),
+            vmem((16, 16, OWN), bf16),
+            vmem((FEATS, 8 * CHUNK), bf16),
+            vmem((rows, FEATS), bf16),
+            vmem((rows, 256), f32),
+            vmem((16, OWN, 256), bf16),
+            vmem((16, OWN, 256), bf16),
+            vmem((5, 64, LEAF), bf16),
+            vmem((3, LEAF, LEAF), f32),
+            vmem((2, 2, 16, 64), bf16),
+            vmem((2, LEAF, 256), f32),
+            vmem((2, LEAF, 256), f32),
+            vmem((2, LEAF, 64), f32),
+            vmem((3, LEAF, 64), f32),
+            vmem((2, 64, 256), f32),
             dma((6,)), dma((16,)), dma((16,)), dma((4, 5)), dma((2, 5)), dma((2, 5)), dma((8, 5)), dma((16,)), dma((16,)),
+            dma((2, 3)), dma((2, 3)), dma((5,)),
         ],
         compiler_params=pltpu.CompilerParams(collective_id=0, has_side_effects=True, vmem_limit_bytes=60 << 20),
-    )(probes, points)
-
-
-def swapped(value, axis, bit):
-    return lax.ppermute(value, axis, [(i, i ^ 1 << bit) for i in range(lax.axis_size(axis))])
-
-
-def couple(row_feats, col_feats, kernel_gain):
-    cross = jnp.dot(row_feats.T, col_feats, precision=exact_mode)
-    row_sq = jnp.sum(row_feats * row_feats, axis=0)
-    col_sq = jnp.sum(col_feats * col_feats, axis=0)
-    feat_count = row_feats.shape[0]
-    return kernel_gain * jnp.exp(
-        (2.0 * cross - row_sq[:, None] - col_sq[None, :]) / (2.0 * feat_count)
-    )
-
-
-def interpolate(stacked, chosen):
-    skeleton = jnp.take(stacked, chosen, axis=0)
-    gram_mat = jnp.dot(skeleton, skeleton.T, precision=exact_mode)
-    damping = 0.05 * jnp.sum(skeleton * skeleton) / chosen.shape[0] + 1e-05
-    factor = jnp.linalg.cholesky(gram_mat + damping * jnp.eye(chosen.shape[0], dtype=stacked.dtype))
-    cross_mat = jnp.dot(stacked, skeleton.T, precision=exact_mode)
-    solved = jax.scipy.linalg.cho_solve((factor, True), cross_mat.T)
-    return (solved.T, skeleton)
-
-
-def leaf_level(leaf_rows, leaf_probes, coords, chosen):
-    interp, skeleton = interpolate(leaf_rows, chosen)
-    reduced = jnp.dot(interp.T, leaf_probes.astype(interp.dtype), precision=exact_mode)
-    picked = jnp.take(coords, chosen, axis=1).astype(jnp.float32)
-    return (interp, (skeleton, reduced, picked))
-
-
-def merge_pair(first_child, second_child, chosen, kernel_gain):
-    first_samples, first_reduced, first_points = first_child
-    second_samples, second_reduced, second_points = second_child
-    upper_rows = first_samples - jnp.dot(
-        couple(first_points, second_points, kernel_gain), second_reduced, precision=exact_mode
-    )
-    lower_rows = second_samples - jnp.dot(
-        couple(second_points, first_points, kernel_gain), first_reduced, precision=exact_mode
-    )
-    stacked = jnp.concatenate([upper_rows, lower_rows], axis=0)
-    interp, skeleton = interpolate(stacked, chosen)
-    reduced = jnp.dot(
-        interp.T, jnp.concatenate([first_reduced, second_reduced], axis=0), precision=exact_mode
-    )
-    joined = jnp.take(jnp.concatenate([first_points, second_points], axis=1), chosen, axis=1)
-    return (interp, (skeleton, reduced, joined))
-
-
-def take_first(values):
-    return values[0]
-
-
-def take_second(values):
-    return values[1]
-
-
-def local(probes, points, leaf_skeleton, skeleton_one, skeleton_two, skeleton_three):
-    feat_count = points.shape[0]
-    own_rows = probes.shape[1]
-    col_pos = lax.axis_index("col")
-    extent = own_rows * lax.axis_size("row") * lax.axis_size("col")
-    kernel_gain = 16.0 / math.sqrt(4 * extent)
-    owned = sample_rows(probes, points.transpose(1, 0, 2), kernel_gain)
-    leaf_count = own_rows // LEAF
-    leaf_rows = owned.reshape(leaf_count, LEAF, -1)
-    leaf_probes = probes[0].reshape(leaf_count, LEAF, -1)
-    leaf_coords = points[:, 0].reshape(feat_count, leaf_count, LEAF).transpose(1, 0, 2)
-    leaf_interp, carried = jax.vmap(leaf_level)(leaf_rows, leaf_probes, leaf_coords, leaf_skeleton)
-    first_child = jax.tree.map(take_first, carried)
-    second_child = jax.tree.map(take_second, carried)
-    interp_one, carried = merge_pair(first_child, second_child, skeleton_one[0], kernel_gain)
-    upper_list = [interp_one]
-    for bit_num in range(2):
-        partner = swapped((carried[0], carried[1], carried[2]), "col", bit_num)
-        mine_first = col_pos >> bit_num & 1 == 0
-        first_child = jax.tree.map(partial(jnp.where, mine_first), carried, partner)
-        second_child = jax.tree.map(partial(jnp.where, mine_first), partner, carried)
-        table_rows = skeleton_two if bit_num == 0 else skeleton_three
-        chosen = lax.dynamic_index_in_dim(table_rows, col_pos // (2 << bit_num), 0, keepdims=False)
-        interp_up, carried = merge_pair(first_child, second_child, chosen, kernel_gain)
-        upper_list.append(interp_up)
-    upper_interp = jnp.stack(upper_list)[:, None]
-    top_state = jnp.stack([carried[0], carried[1]])[:, None]
-    return (leaf_interp, upper_interp, top_state)
+    )(probes, points.transpose(1, 0, 2), leaf_skeleton, skeleton_one, skeleton_two, skeleton_three)
+    return leaf_interp, upper_interp[:, None], top_state[:, None]
 
 
 def solution(mesh):

time: 174 us -> 103 us (0.59)
  other arithmetic: 63.9 us -> 0 us
  Pallas kernels: 71.7 us -> 97.4 us
  starting transfers between devices: 10 us -> 0 us
  matrix products: 7.05 us -> 0 us
  waiting for transfers between devices: 7.03 us -> 0 us
  local copies, waits for them, and re-layouts: 11.1 us -> 4.6 us
  between operations: 3.18 us -> 0.65 us
    another operation x23 -> x0, other arithmetic: 58.7 us -> none  [the longest x13 31.4 us: interpolate(): jnp.linalg.cholesky(gram_mat + damping * jnp.eye(chosen.shape[0], dtype=s...]
    pallas_call x1, Pallas kernels: 71.7 us -> 97.4 us  [local(): pl.pallas_call(partial(hss_kernel, kernel_gain), out_shape=(jax.ShapeDtyp...]
    ppermute x6 -> x0, starting transfers between devices: 10 us -> none  [swapped(): lax.ppermute(value, axis, [(i, i ^ 1 << bit) for i in range(lax.axis_size...]
    ppermute x6 -> x0, waiting for transfers between devices: 7.03 us -> none  [swapped(): lax.ppermute(value, axis, [(i, i ^ 1 << bit) for i in range(lax.axis_size...]
    gather x9 -> x0, local copies, waits for them, and re-layouts: 6.36 us -> none  [the longest x5 3.96 us: interpolate(): skeleton = jnp.take(stacked, chosen, axis=0)]
    dot_general x24 -> x0, matrix products: 5.31 us -> none  [the longest x4 1.2 us: interpolate(): cross_mat = jnp.dot(stacked, skeleton.T, precision=exact_mode)]
    reduce_sum x6 -> x0, other arithmetic: 1.93 us -> none  [the longest x3 1.56 us: interpolate(): damping = 0.05 * jnp.sum(skeleton * skeleton) / chosen.shape[0] + 1e-05]
    unnamed x11 -> x8, local copies, waits for them, and re-layouts: 3.31 us -> 4.6 us
  transfers between devices with their start and end apart: 6 -> 0, of which waited for: 3 -> 0; matrix products, arithmetic and copies ran while one was open for 10% -> 0% of each run, Pallas kernels for 0% -> 0%
where the time goes in v2:
time: 103 us
  Pallas kernels  97.4 us (95%)
  local copies, waits for them, and re-layouts  4.6 us (4%)
    pallas_call x1, Pallas kernels, local(): pl.pallas_call(partial(hss_kernel, kernel_gain), out_shape=(jax.ShapeDtyp...  97.4 us
    unnamed x8, local copies, waits for them, and re-layouts  4.6 us

profile of v2, /device:TPU:0, one launch (start us, length us, event | category | flops | bytes accessed | tf_op | source)
XLA Modules:
  0.0 102.7 jit_solution(13717047622916231911)
XLA Ops:
  0.6 1.4 %copy.14 = bf16[16,4,256]{2,0,1:T(8,128)(2,1)} copy(bf16[16,4,256]{2,1,0:T(4,128)(2,1)} %param.7) | data formatting | bytes 65536 | tf_op args[1]
  2.0 97.4 %shard_map.85 = (f32[2,128,64]{2,1,0:T(8,128)}, f32[3,128,64]{2,1,0:T(8,128)}, f32[2,64,256]{2,1,0:T(8,128)}) custom-call(bf16[4,256,256]{2,1,0:T(8,128)(2,1)} %probes.1, bf16[4,16,256]{2,1,0:T(8,128)(2,1)} %bitcast.8, s32[2,64]{1,0:T(2,128)} %chosen_leaf.1, s32[1,64]{1,0:T(1,128)} %chosen_one.1, s32[8,64]{1,0:T(8,128)} %chosen_two.1, s32[4,64]{1,0:T(4,128)} %chosen_three.1), custom_call_target="tpu_custom_call" | custom-call | tf_op jit(solution)/shard_map/pallas_call | solution.py:392
  99.4 0.0 copy-start
  99.5 1.7 %copy.10 = f32[2,128,64]{1,2,0:T(8,128)} copy(f32[2,128,64]{2,1,0:T(8,128)} %get-tuple-element.9) | data formatting | bytes 131072
  101.1 0.0 copy-done
  101.1 0.0 copy-start.1
  101.1 0.8 copy.11
  101.9 0.1 copy-done.1
  102.0 0.7 copy.16
Async XLA Ops:
  99.4 1.7 %copy-start = (f32[3,128,64]{2,1,0:T(8,128)S(1)}, f32[3,128,64]{2,1,0:T(8,128)}, u32[]{:S(2)}) copy-start(f32[3,128,64]{2,1,0:T(8,128)} %get-tuple-element.7) | copy-start | bytes 294916
  101.1 0.9 copy-start.1

commit v3 on v2

--- a/solution.py
+++ b/solution.py
@@ -107,10 +107,6 @@
     return jnp.where(child == other, 0.0, jnp.exp2(power))
 
 
-def spread(i):
-    return lax.rem(2 + i + lax.div(i * (i - 1), 2), SIDE)
-
-
 def hss_kernel(gain, probes, points, chosen_leaf, chosen_one, chosen_two, chosen_three, leaf_out, upper_out, top_out,
                prb, pts, rpts, colf, rowf, acc, outbox, inbox, picks, square, pair_p, pair_z, pair_r, leaf_x, upper_x, top_x,
                loc_sem, rp_send, rp_recv, chip_send, up_send, down_send, got, box_send, box_recv, pair_send, pair_recv, out_sem):
@@ -122,10 +118,12 @@
     partner = y * 2 + 1 - core
 
     local = [pltpu.make_async_copy(probes.at[q], prb.at[pl.ds(q * OWN, OWN)], loc_sem.at[q]) for q in range(4)]
-    local.append(pltpu.make_async_copy(points, pts.at[0], loc_sem.at[4]))
-    local.append(pltpu.make_async_copy(points.at[0], rpts.at[0], loc_sem.at[5]))
     for copy in local:
         copy.start()
+    feats = points[...].astype(jnp.float32)
+    for q in range(4):
+        pts[0, q] = feats[:, q, :].astype(jnp.bfloat16)
+    rpts[0] = pts[0, 0]
 
     def peer_col(j, sign):
         dx, dz = j // SIDE, lax.rem(j, SIDE)
@@ -305,7 +303,7 @@
             device_id=(row, peer_col(j, -1)), device_id_type=MESH)
 
     def last_block(i, _):
-        j = spread(i // SIDE) * SIDE + spread(lax.rem(i, SIDE))
+        j = lax.rem(13 * i + 13, 16)
         tile, rows = block(j, EARLY, 8)
         total = acc[at(j), :] + jnp.dot(tile, rows, preferred_element_type=jnp.float32)
         outbox[j] = total.astype(jnp.bfloat16)
@@ -317,7 +315,7 @@
     acc[pl.ds(0, OWN), :] += jnp.dot(tile, rows, preferred_element_type=jnp.float32)
 
     def take(i, _):
-        j = spread(i // SIDE) * SIDE + spread(lax.rem(i, SIDE))
+        j = lax.rem(13 * i + 13, 16)
         box_copy(j).wait_recv()
         acc[pl.ds(0, OWN), :] += inbox[j].astype(jnp.float32)
         return 0
@@ -332,7 +330,7 @@
     for leaf, value in enumerate(solved):
         rows = prb[pl.ds(leaf * LEAF, LEAF), :]
         reduced.append(jnp.dot(jnp.concatenate(split(value), axis=1), jnp.concatenate([rows] * 3, axis=0), preferred_element_type=jnp.float32))
-        leaf_x[leaf] = value.T
+        leaf_x[leaf] = value
     leave(leaf_x, leaf_out, out_sem.at[0])
     below, weights = jnp.concatenate(kept, axis=0), jnp.concatenate(reduced, axis=0)
     for level in range(3):
@@ -356,7 +354,7 @@
         else:
             pair_r[level, pl.ds(pl.multiple_of(bits[level] * 64, 64), 64), :] = value
             pair_copy(level, 2).start()
-        upper_x[level] = solved[0].T
+        upper_x[level] = solved[0]
         leave(upper_x.at[level], upper_out.at[level], out_sem.at[1 + level])
 
     def drain(j, _):
@@ -392,11 +390,11 @@
     leaf_interp, upper_interp, top_state = pl.pallas_call(
         partial(hss_kernel, kernel_gain),
         out_shape=(
-            jax.ShapeDtypeStruct((2, LEAF, 64), f32),
-            jax.ShapeDtypeStruct((3, LEAF, 64), f32),
+            jax.ShapeDtypeStruct((2, 64, LEAF), f32),
+            jax.ShapeDtypeStruct((3, 64, LEAF), f32),
             jax.ShapeDtypeStruct((2, 64, 256), f32),
         ),
-        in_specs=[outside, outside, inside, inside, inside, inside],
+        in_specs=[outside, inside, inside, inside, inside, inside],
         out_specs=(outside, outside, outside),
         scratch_shapes=[
             vmem((8 * CHUNK, 256), bf16),
@@ -412,15 +410,15 @@
             vmem((2, 2, 16, 64), bf16),
             vmem((2, LEAF, 256), f32),
             vmem((2, LEAF, 256), f32),
-            vmem((2, LEAF, 64), f32),
-            vmem((3, LEAF, 64), f32),
+            vmem((2, 64, LEAF), f32),
+            vmem((3, 64, LEAF), f32),
             vmem((2, 64, 256), f32),
-            dma((6,)), dma((16,)), dma((16,)), dma((4, 5)), dma((2, 5)), dma((2, 5)), dma((8, 5)), dma((16,)), dma((16,)),
+            dma((4,)), dma((16,)), dma((16,)), dma((4, 5)), dma((2, 5)), dma((2, 5)), dma((8, 5)), dma((16,)), dma((16,)),
             dma((2, 3)), dma((2, 3)), dma((5,)),
         ],
         compiler_params=pltpu.CompilerParams(collective_id=0, has_side_effects=True, vmem_limit_bytes=60 << 20),
-    )(probes, points.transpose(1, 0, 2), leaf_skeleton, skeleton_one, skeleton_two, skeleton_three)
-    return leaf_interp, upper_interp[:, None], top_state[:, None]
+    )(probes, points, leaf_skeleton, skeleton_one, skeleton_two, skeleton_three)
+    return leaf_interp.swapaxes(1, 2), upper_interp.swapaxes(1, 2)[:, None], top_state[:, None]
 
 
 def solution(mesh):

time: 103 us -> 95.7 us (0.929)
  Pallas kernels: 97.4 us -> 92 us
  local copies, waits for them, and re-layouts: 4.6 us -> 2.82 us
    pallas_call x1, Pallas kernels: 97.4 us -> 92 us  [local(): pl.pallas_call(partial(hss_kernel, kernel_gain), out_shape=(jax.ShapeDtyp...]
    unnamed x8 -> x7, local copies, waits for them, and re-layouts: 4.6 us -> 2.82 us
where the time goes in v3:
time: 95.7 us; the launch traced here: 95.5 us
  Pallas kernels  92 us (96%)
  local copies, waits for them, and re-layouts  2.82 us (3%)
    pallas_call x1, Pallas kernels, local(): pl.pallas_call(partial(hss_kernel, kernel_gain), out_shape=(jax.ShapeDtyp...  92 us
    unnamed x7, local copies, waits for them, and re-layouts  2.82 us

profile of v3, /device:TPU:0, one launch (start us, length us, event | category | flops | bytes accessed | tf_op | source)
XLA Modules:
  0.0 95.5 jit_solution(9419666006004633180)
XLA Ops:
  0.6 92.0 %shard_map.85 = (f32[2,64,128]{2,1,0:T(8,128)}, f32[3,64,128]{2,1,0:T(8,128)}, f32[2,64,256]{2,1,0:T(8,128)}) custom-call(bf16[4,256,256]{2,1,0:T(8,128)(2,1)} %probes.1, bf16[16,4,256]{2,1,0:T(4,128)(2,1)} %points.1, s32[2,64]{1,0:T(2,128)} %chosen_leaf.1, s32[1,64]{1,0:T(1,128)} %chosen_one.1, s32[8,64]{1,0:T(8,128)} %chosen_two.1, s32[4,64]{1,0:T(4,128)} %chosen_three.1), custom_call_target="tpu_custom_call" | custom-call | tf_op jit(solution)/shard_map/pallas_call | solution.py:390
  92.7 0.0 copy-start.1
  92.7 0.0 copy-start
  92.7 1.5 %copy.14 = f32[2,128,64]{1,2,0:T(8,128)} copy(f32[2,128,64]{1,2,0:T(8,128)} %bitcast.11) | data formatting | bytes 131072
  94.2 0.0 copy-done.1
  94.2 0.6 copy.15
  94.9 0.0 copy-done
  94.9 0.7 copy.16
Async XLA Ops:
  92.7 1.5 %copy-start.1 = (f32[3,64,128]{2,1,0:T(8,128)S(1)}, f32[3,64,128]{2,1,0:T(8,128)}, u32[]{:S(2)}) copy-start(f32[3,64,128]{2,1,0:T(8,128)} %get-tuple-element.7) | copy-start | bytes 294916
  92.7 2.2 %copy-start = (f32[2,64,256]{2,1,0:T(8,128)S(1)}, f32[2,64,256]{2,1,0:T(8,128)}, u32[]{:S(2)}) copy-start(f32[2,64,256]{2,1,0:T(8,128)} %get-tuple-element.8) | copy-start | bytes 393220

commit v4 on v3

--- a/solution.py
+++ b/solution.py
@@ -1,4 +1,4 @@
-from functools import partial
+import functools
 import math
 
 import jax
@@ -17,7 +17,8 @@
 CHUNK = 4 * OWN
 FEATS = 64
 PLACE = {(0, 0): 0, (0, 1): 1, (1, 0): 2, (3, 0): 3, (1, 1): 4, (3, 1): 5, (2, 0): 6, (2, 1): 7}
-EARLY = 3
+EARLY = 4
+MIDWAY = 3
 
 
 def pieces(value):
@@ -57,11 +58,12 @@
 def eliminate(systems):
     width = systems[0].shape[1]
     sub = lax.broadcasted_iota(jnp.int32, (8, 1), 0)
-    systems = [[m[8 * i:8 * i + 8, :] for i in range(8)] for m in systems]
+    pivots = [m[0:8, :] for m in systems]
+    systems = list(systems)
     for b in range(8):
-        for m in systems:
-            cols = [[jnp.broadcast_to(m[i][:, 8 * b + j:8 * b + j + 1], (8, 128)) for j in range(8)] for i in range(8)]
-            p, lead = m[b], list(cols[b])
+        for s, m in enumerate(systems):
+            p = pivots[s]
+            lead = [jnp.broadcast_to(p[:, 8 * b + j:8 * b + j + 1], (8, 128)) for j in range(8)]
             for k in range(8):
                 inv = 1.0 / lead[k][k:k + 1, :]
                 f = lead[k] * inv
@@ -70,14 +72,21 @@
                 for j in range(k + 1, 8):
                     q = lead[j][k:k + 1, :]
                     lead[j] = jnp.where(sub == k, q * inv, lead[j] - f * q)
-            m[b] = p
-            for i in range(8):
-                if i != b:
-                    total = m[i]
-                    for k in range(8):
-                        total = total - wide(cols[i][k], width) * p[k:k + 1, :]
-                    m[i] = total
-    return [jnp.concatenate(m, axis=0)[:, 64:] for m in systems]
+            if b < 7:
+                after = m[8 * b + 8:8 * b + 16, :]
+                ahead = after
+                for k in range(8):
+                    ahead = ahead - wide(jnp.broadcast_to(after[:, 8 * b + k:8 * b + k + 1], (8, 128)), width) * p[k:k + 1, :]
+                pivots[s] = ahead
+            ch, cm, cl = split(m[:, 8 * b:8 * b + 8])
+            ph, pm, low = split(p)
+            change = jnp.dot(jnp.concatenate([ch, ch, cm, ch, cl, cm], axis=1), jnp.concatenate([ph, pm, ph, low, ph, pm], axis=0),
+                             preferred_element_type=jnp.float32)
+            rest = m - change
+            systems[s] = jnp.concatenate(
+                [p if i == b else pivots[s] if i == b + 1 else rest[8 * i:8 * i + 8, :] for i in range(8)], axis=0)
+    return [m[:, 64:] for m in systems]
+
 
 def interpolate(stacked, picks, keep=None):
     systems, kept = [], []
@@ -108,8 +117,8 @@
 
 
 def hss_kernel(gain, probes, points, chosen_leaf, chosen_one, chosen_two, chosen_three, leaf_out, upper_out, top_out,
-               prb, pts, rpts, colf, rowf, acc, outbox, inbox, picks, square, pair_p, pair_z, pair_r, leaf_x, upper_x, top_x,
-               loc_sem, rp_send, rp_recv, chip_send, up_send, down_send, got, box_send, box_recv, pair_send, pair_recv, out_sem):
+               prb, pts, rpts, colf, rowf, acc, outbox, inbox, sum_out, sum_in, picks, square, pair_p, pair_z, pair_r, pair_out, pair_in, leaf_x, upper_x, top_x,
+               loc_sem, rp_send, rp_recv, chip_send, up_send, down_send, got, box_send, box_recv, sum_send, sum_recv, pair_send, pair_recv, out_sem):
     row, col = lax.axis_index("row"), lax.axis_index("col")
     y, core = row // 2, lax.rem(row, 2)
     x, z = col // SIDE, lax.rem(col, SIDE)
@@ -125,19 +134,37 @@
         pts[0, q] = feats[:, q, :].astype(jnp.bfloat16)
     rpts[0] = pts[0, 0]
 
-    def peer_col(j, sign):
-        dx, dz = j // SIDE, lax.rem(j, SIDE)
-        return lax.rem(x + sign * dx + SIDE, SIDE) * SIDE + lax.rem(z + sign * dz + SIDE, SIDE)
+    def shifted(dx, dz):
+        return lax.rem(x + dx + SIDE, SIDE) * SIDE + lax.rem(z + dz + SIDE, SIDE)
+
+    def far(i):
+        return 1 + i, 1 + lax.rem(i // 3 + 1, 3), 1 + lax.rem(i + 1, 3)
+
+    def line(k, half):
+        d = 1 + lax.rem(k + 1, 3)
+        return (10 + 2 * k, 0, d) if half == 0 else (11 + 2 * k, d, 0)
 
     barrier = pltpu.get_barrier_semaphore()
     for other in (up, down, partner):
         pl.semaphore_signal(barrier, inc=1, device_id=(other, col), device_id_type=MESH)
 
-    def greet(j, _):
-        pl.semaphore_signal(barrier, inc=1, device_id=(row, peer_col(j, 1)), device_id_type=MESH)
-        return 0
-
-    lax.fori_loop(1, 16, greet, 0)
+    def each_peer(action):
+        def on_axis(k, _):
+            for half in range(2):
+                action(*line(k, half))
+            return 0
+
+        def off_axis(i, _):
+            action(*far(i))
+            return 0
+
+        lax.fori_loop(0, 3, on_axis, 0)
+        lax.fori_loop(0, 9, off_axis, 0)
+
+    def greet(slot, dx, dz):
+        pl.semaphore_signal(barrier, inc=1, device_id=(row, shifted(dx, dz)), device_id_type=MESH)
+
+    each_peer(greet)
     for copy in local:
         copy.wait()
 
@@ -145,9 +172,13 @@
 
     def pair_copy(level, kind):
         bit = bits[level]
-        ref = pair_p.at[level, bit] if kind == 0 else (pair_z, pair_r)[kind - 1].at[level, pl.ds(pl.multiple_of(bit * 64, 64), 64)]
+        if kind == 2:
+            src_ref, dst_ref = pair_out.at[level], pair_in.at[level]
+        else:
+            src_ref = pair_p.at[level, bit] if kind == 0 else pair_z.at[level, pl.ds(pl.multiple_of(bit * 64, 64), 64)]
+            dst_ref = src_ref
         return pltpu.make_async_remote_copy(
-            src_ref=ref, dst_ref=ref, send_sem=pair_send.at[level, kind], recv_sem=pair_recv.at[level, kind],
+            src_ref=src_ref, dst_ref=dst_ref, send_sem=pair_send.at[level, kind], recv_sem=pair_recv.at[level, kind],
             device_id=(row, col + (1 - 2 * bit) * (level + 1)), device_id_type=MESH)
 
     for leaf in range(2):
@@ -171,14 +202,10 @@
     child_points(0, jnp.concatenate([picked(pts[0, 0, :, leaf * LEAF:(leaf + 1) * LEAF], picks[leaf]) for leaf in range(2)], axis=1))
     pl.semaphore_wait(barrier, 18)
 
-    def row_copy(j):
+    def row_copy(slot, dx, dz):
         return pltpu.make_async_remote_copy(
-            src_ref=rpts.at[0], dst_ref=rpts.at[j], send_sem=rp_send.at[j], recv_sem=rp_recv.at[j],
-            device_id=(row, peer_col(j, 1)), device_id_type=MESH)
-
-    def send_row(j, _):
-        row_copy(j).start()
-        return 0
+            src_ref=rpts.at[0], dst_ref=rpts.at[slot], send_sem=rp_send.at[slot], recv_sem=rp_recv.at[slot],
+            device_id=(row, shifted(dx, dz)), device_id_type=MESH)
 
     def piece_copy(src, dst, q, sem, target):
         src_ref = pts.at[src] if q == 4 else prb.at[pl.ds(src * CHUNK + q * OWN, OWN)]
@@ -203,7 +230,7 @@
     on_chip(0, 4).start()
     upward(0, 4).start()
     downward(0, 4).start()
-    lax.fori_loop(1, 16, send_row, 0)
+    each_peer(lambda slot, dx, dz: row_copy(slot, dx, dz).start())
     pair_copy(0, 0).start()
     for q in range(4):
         on_chip(0, q).start()
@@ -226,14 +253,13 @@
         stacked = jnp.concatenate([*pieces(feats * (LOG2E / 16)), extra_rows(pieces(bias), ones)], axis=0)
         rowf[pl.ds(pl.multiple_of(j * OWN, OWN), OWN), :] = stacked.T.astype(jnp.bfloat16)
 
-    def block(j, first, last):
-        rows = rowf[pl.ds(pl.multiple_of(j * OWN, OWN), OWN), :]
+    def at(slot, count):
+        return pl.ds(pl.multiple_of(slot * OWN, OWN), count * OWN)
+
+    def partial(slot, count, first, last):
         cols = pl.ds(first * CHUNK, (last - first) * CHUNK)
-        power = jnp.dot(rows, colf[:, cols], preferred_element_type=jnp.float32)
-        return jnp.exp2(power).astype(jnp.bfloat16), prb[cols, :]
-
-    def at(j):
-        return pl.ds(pl.multiple_of(j * OWN, OWN), OWN)
+        power = jnp.dot(rowf[at(slot, count), :], colf[:, cols], preferred_element_type=jnp.float32)
+        return jnp.dot(jnp.exp2(power).astype(jnp.bfloat16), prb[cols, :], preferred_element_type=jnp.float32)
 
     col_features(0)
     row_features(0)
@@ -245,29 +271,35 @@
     for q in (4, 0, 1, 2, 3):
         arrived(0, 1, q)
     col_features(1)
-    tile, rows = block(0, 1, 2)
-    acc[pl.ds(0, OWN), :] = own_sum + jnp.dot(tile, rows, preferred_element_type=jnp.float32)
-
-    def near_block(j, _):
-        row_copy(j).wait_recv()
-        row_features(j)
-        tile, rows = block(j, 0, 2)
-        acc[at(j), :] = jnp.dot(tile, rows, preferred_element_type=jnp.float32)
-
-        @pl.when(j == 10)
-        def _():
-            for q in (4, 0, 1):
-                arrived(1, 0, q)
-                upward(1, q).start()
-                on_chip(1, q).start()
-            for q in (4, 2, 3):
-                arrived(3, 0, q)
-                if q != 4:
-                    downward(3, q).start()
-                on_chip(3, q).start()
+    acc[at(0, 1), :] = own_sum + partial(0, 1, 1, 2)
+
+    def near_line(k, _):
+        for half in range(2):
+            slot, dx, dz = line(k, half)
+            row_copy(slot, dx, dz).wait_recv()
+            row_features(slot)
+        acc[at(10 + 2 * k, 2), :] = partial(10 + 2 * k, 2, 0, 2)
         return 0
 
-    lax.fori_loop(1, 16, near_block, 0)
+    def near_far(i, _):
+        for e in range(3):
+            slot, dx, dz = far(3 * i + e)
+            row_copy(slot, dx, dz).wait_recv()
+            row_features(slot)
+        acc[at(1 + 3 * i, 3), :] = partial(1 + 3 * i, 3, 0, 2)
+        return 0
+
+    lax.fori_loop(0, 3, near_line, 0)
+    for q in (4, 0, 1):
+        arrived(1, 0, q)
+        upward(1, q).start()
+        on_chip(1, q).start()
+    for q in (4, 2, 3):
+        arrived(3, 0, q)
+        if q != 4:
+            downward(3, q).start()
+        on_chip(3, q).start()
+    lax.fori_loop(0, 3, near_far, 0)
     for q, r in ((2, 0), (3, 1)):
         arrived(1, 0, q)
         on_chip(1, q).start()
@@ -278,18 +310,17 @@
     child_points(1, pair_points(0))
     pair_copy(1, 0).start()
 
-    def mid_block(j, _):
-        tile, rows = block(j, 2, EARLY)
-        acc[at(j), :] += jnp.dot(tile, rows, preferred_element_type=jnp.float32)
-
-        @pl.when(j == 12)
+    def middle(i, _):
+        @pl.when(i == MIDWAY)
         def _():
             for q in (4, 0, 2, 1, 3):
                 arrived(2, 0, q)
                 on_chip(2, q).start()
+
+        acc[at(4 * i, 4), :] += partial(4 * i, 4, 2, EARLY)
         return 0
 
-    lax.fori_loop(0, 16, mid_block, 0)
+    lax.fori_loop(0, 4, middle, 0)
     child_points(2, pair_points(1))
     for dy in (1, 3, 2):
         for q in (4, 0, 1, 2, 3):
@@ -297,30 +328,59 @@
     for place in range(EARLY, 8):
         col_features(place)
 
-    def box_copy(j):
+    def box_copy(half, slot, dx, dz):
+        target = shifted(-dx, 0) if half == 0 else shifted(0, -dz)
         return pltpu.make_async_remote_copy(
-            src_ref=outbox.at[j], dst_ref=inbox.at[j], send_sem=box_send.at[j], recv_sem=box_recv.at[j],
-            device_id=(row, peer_col(j, -1)), device_id_type=MESH)
-
-    def last_block(i, _):
-        j = lax.rem(13 * i + 13, 16)
-        tile, rows = block(j, EARLY, 8)
-        total = acc[at(j), :] + jnp.dot(tile, rows, preferred_element_type=jnp.float32)
-        outbox[j] = total.astype(jnp.bfloat16)
-        box_copy(j).start()
+            src_ref=outbox.at[slot, half], dst_ref=inbox.at[half, slot],
+            send_sem=box_send.at[half, slot], recv_sem=box_recv.at[half, slot],
+            device_id=(row, target), device_id_type=MESH)
+
+    def sum_copy(half, k):
+        _, dx, dz = line(k, half)
+        return pltpu.make_async_remote_copy(
+            src_ref=sum_out.at[half, k], dst_ref=sum_in.at[half, k], send_sem=sum_send.at[half, k], recv_sem=sum_recv.at[half, k],
+            device_id=(row, shifted(-dx, -dz)), device_id_type=MESH)
+
+    def half_of(value, half):
+        return value[:, half * 128:(half + 1) * 128]
+
+    def far_blocks(i, _):
+        total = acc[at(1 + 3 * i, 3), :] + partial(1 + 3 * i, 3, EARLY, 8)
+        for e in range(3):
+            slot, dx, dz = far(3 * i + e)
+            for half in range(2):
+                outbox[slot, half] = half_of(total[e * OWN:(e + 1) * OWN], half).astype(jnp.bfloat16)
+                box_copy(half, slot, dx, dz).start()
         return 0
 
-    lax.fori_loop(0, 15, last_block, 0)
-    tile, rows = block(0, EARLY, 8)
-    acc[pl.ds(0, OWN), :] += jnp.dot(tile, rows, preferred_element_type=jnp.float32)
-
-    def take(i, _):
-        j = lax.rem(13 * i + 13, 16)
-        box_copy(j).wait_recv()
-        acc[pl.ds(0, OWN), :] += inbox[j].astype(jnp.float32)
+    def line_blocks(k, _):
+        total = acc[at(10 + 2 * k, 2), :] + partial(10 + 2 * k, 2, EARLY, 8)
+        for half in range(2):
+            slot, dx, dz = line(k, half)
+            mine, other = total[half * OWN:(half + 1) * OWN], 1 - half
+            outbox[slot, other] = half_of(mine, other).astype(jnp.bfloat16)
+            box_copy(other, slot, dx, dz).start()
+            summed = half_of(mine, half)
+            for e in range(3):
+                source, dx, dz = far(3 * e + k if half == 0 else 3 * k + e)
+                box_copy(half, source, dx, dz).wait_recv()
+                summed = summed + inbox[half, source].astype(jnp.float32)
+            sum_out[half, k] = summed
+            sum_copy(half, k).start()
         return 0
 
-    lax.fori_loop(0, 15, take, 0)
+    lax.fori_loop(0, 3, far_blocks, 0)
+    lax.fori_loop(0, 3, line_blocks, 0)
+    total = acc[at(0, 1), :] + partial(0, 1, EARLY, 8)
+    for half in range(2):
+        summed = half_of(total, half)
+        for k in range(3):
+            slot, dx, dz = line(k, 1 - half)
+            box_copy(half, slot, dx, dz).wait_recv()
+            summed = summed + inbox[half, slot].astype(jnp.float32)
+            sum_copy(half, k).wait_recv()
+            summed = summed + sum_in[half, k]
+        acc[pl.ds(0, OWN), half * 128:(half + 1) * 128] = summed
 
     def leave(src, dst, sem):
         pltpu.make_async_copy(src, dst, sem).start()
@@ -337,6 +397,7 @@
         if level > 0:
             pair_copy(level - 1, 1).wait_recv()
             pair_copy(level - 1, 2).wait_recv()
+            pair_r[level - 1, pl.ds(pl.multiple_of(64 - bits[level - 1] * 64, 64), 64), :] = pair_in[level - 1].astype(jnp.float32)
             below, weights = pair_z[level - 1], pair_r[level - 1]
 
         def keep(value):
@@ -352,17 +413,27 @@
             top_x[1] = value
             leave(top_x, top_out, out_sem.at[4])
         else:
+            pair_out[level] = value.astype(jnp.bfloat16)
+            pair_copy(level, 2).start()
             pair_r[level, pl.ds(pl.multiple_of(bits[level] * 64, 64), 64), :] = value
-            pair_copy(level, 2).start()
         upper_x[level] = solved[0]
         leave(upper_x.at[level], upper_out.at[level], out_sem.at[1 + level])
 
-    def drain(j, _):
-        row_copy(j).wait_send()
-        box_copy(j).wait_send()
+    def drain(slot, dx, dz):
+        row_copy(slot, dx, dz).wait_send()
+
+    each_peer(drain)
+
+    def drain_far(i, _):
+        for half in range(2):
+            box_copy(half, *far(i)).wait_send()
         return 0
 
-    lax.fori_loop(1, 16, drain, 0)
+    lax.fori_loop(0, 9, drain_far, 0)
+    for k in range(3):
+        for half in range(2):
+            box_copy(half, *line(k, 1 - half)).wait_send()
+            sum_copy(half, k).wait_send()
     for q in range(5):
         for dy in range(4):
             on_chip(dy, q).wait_send()
@@ -388,7 +459,7 @@
     rows = 16 * OWN
     outside, inside = pl.BlockSpec(memory_space=pl.ANY), pl.BlockSpec(memory_space=vmem)
     leaf_interp, upper_interp, top_state = pl.pallas_call(
-        partial(hss_kernel, kernel_gain),
+        functools.partial(hss_kernel, kernel_gain),
         out_shape=(
             jax.ShapeDtypeStruct((2, 64, LEAF), f32),
             jax.ShapeDtypeStruct((3, 64, LEAF), f32),
@@ -403,17 +474,21 @@
             vmem((FEATS, 8 * CHUNK), bf16),
             vmem((rows, FEATS), bf16),
             vmem((rows, 256), f32),
-            vmem((16, OWN, 256), bf16),
-            vmem((16, OWN, 256), bf16),
+            vmem((16, 2, OWN, 128), bf16),
+            vmem((2, 16, OWN, 128), bf16),
+            vmem((2, 3, OWN, 128), f32),
+            vmem((2, 3, OWN, 128), f32),
             vmem((5, 64, LEAF), bf16),
             vmem((3, LEAF, LEAF), f32),
             vmem((2, 2, 16, 64), bf16),
             vmem((2, LEAF, 256), f32),
             vmem((2, LEAF, 256), f32),
+            vmem((2, 64, 256), bf16),
+            vmem((2, 64, 256), bf16),
             vmem((2, 64, LEAF), f32),
             vmem((3, 64, LEAF), f32),
             vmem((2, 64, 256), f32),
-            dma((4,)), dma((16,)), dma((16,)), dma((4, 5)), dma((2, 5)), dma((2, 5)), dma((8, 5)), dma((16,)), dma((16,)),
+            dma((4,)), dma((16,)), dma((16,)), dma((4, 5)), dma((2, 5)), dma((2, 5)), dma((8, 5)), dma((2, 16)), dma((2, 16)), dma((2, 3)), dma((2, 3)),
             dma((2, 3)), dma((2, 3)), dma((5,)),
         ],
         compiler_params=pltpu.CompilerParams(collective_id=0, has_side_effects=True, vmem_limit_bytes=60 << 20),

time: 95.7 us -> 87.3 us (0.912)
  Pallas kernels: 92 us -> 83.6 us
    pallas_call x1, Pallas kernels: 92 us -> 83.6 us  [local(): pl.pallas_call(functools.partial(hss_kernel, kernel_gain), out_shape=(jax...]
where the time goes in v4:
time: 87.3 us; the launch traced here: 87.1 us
  Pallas kernels  83.6 us (96%)
  local copies, waits for them, and re-layouts  2.82 us (3%)
    pallas_call x1, Pallas kernels, local(): pl.pallas_call(functools.partial(hss_kernel, kernel_gain), out_shape=(jax...  83.6 us
    unnamed x7, local copies, waits for them, and re-layouts  2.82 us

profile of v4, /device:TPU:0, one launch (start us, length us, event | category | flops | bytes accessed | tf_op | source)
XLA Modules:
  0.0 87.1 jit_solution(11632945241459643373)
XLA Ops:
  0.6 83.6 %shard_map.85 = (f32[2,64,128]{2,1,0:T(8,128)}, f32[3,64,128]{2,1,0:T(8,128)}, f32[2,64,256]{2,1,0:T(8,128)}) custom-call(bf16[4,256,256]{2,1,0:T(8,128)(2,1)} %probes.1, bf16[16,4,256]{2,1,0:T(4,128)(2,1)} %points.1, s32[2,64]{1,0:T(2,128)} %chosen_leaf.1, s32[1,64]{1,0:T(1,128)} %chosen_one.1, s32[8,64]{1,0:T(8,128)} %chosen_two.1, s32[4,64]{1,0:T(4,128)} %chosen_three.1), custom_call_target="tpu_custom_call" | custom-call | tf_op jit(solution)/shard_map/pallas_call | solution.py:461
  84.3 0.0 copy-start.1
  84.3 0.0 copy-start
  84.3 1.5 %copy.14 = f32[2,128,64]{1,2,0:T(8,128)} copy(f32[2,128,64]{1,2,0:T(8,128)} %bitcast.11) | data formatting | bytes 131072
  85.8 0.0 copy-done.1
  85.8 0.6 copy.15
  86.5 0.0 copy-done
  86.5 0.7 copy.16
Async XLA Ops:
  84.3 1.5 %copy-start.1 = (f32[3,64,128]{2,1,0:T(8,128)S(1)}, f32[3,64,128]{2,1,0:T(8,128)}, u32[]{:S(2)}) copy-start(f32[3,64,128]{2,1,0:T(8,128)} %get-tuple-element.7) | copy-start | bytes 294916
  84.3 2.2 %copy-start = (f32[2,64,256]{2,1,0:T(8,128)S(1)}, f32[2,64,256]{2,1,0:T(8,128)}, u32[]{:S(2)}) copy-start(f32[2,64,256]{2,1,0:T(8,128)} %get-tuple-element.8) | copy-start | bytes 393220

commit v5 on v4

--- a/solution.py
+++ b/solution.py
@@ -116,9 +116,10 @@
     return jnp.where(child == other, 0.0, jnp.exp2(power))
 
 
-def hss_kernel(gain, probes, points, chosen_leaf, chosen_one, chosen_two, chosen_three, leaf_out, upper_out, top_out,
-               prb, pts, rpts, colf, rowf, acc, outbox, inbox, sum_out, sum_in, picks, square, pair_p, pair_z, pair_r, pair_out, pair_in, leaf_x, upper_x, top_x,
+def hss_kernel(gain, probes, points, table_leaf, table_one, table_two, table_three, leaf_out, upper_out, top_out,
+               raw, chosen_leaf, chosen_one, chosen_two, chosen_three, prb, pts, rpts, colf, rowf, acc, outbox, inbox, sum_out, sum_in, picks, square, pair_p, pair_z, pair_r, pair_out, pair_in, leaf_x, upper_x, top_x,
                loc_sem, rp_send, rp_recv, chip_send, up_send, down_send, got, box_send, box_recv, sum_send, sum_recv, pair_send, pair_recv, out_sem):
+    tables = (table_leaf, table_one, table_two, table_three)
     row, col = lax.axis_index("row"), lax.axis_index("col")
     y, core = row // 2, lax.rem(row, 2)
     x, z = col // SIDE, lax.rem(col, SIDE)
@@ -126,14 +127,6 @@
     down = lax.rem(y + 3, SIDE) * 2 + core
     partner = y * 2 + 1 - core
 
-    local = [pltpu.make_async_copy(probes.at[q], prb.at[pl.ds(q * OWN, OWN)], loc_sem.at[q]) for q in range(4)]
-    for copy in local:
-        copy.start()
-    feats = points[...].astype(jnp.float32)
-    for q in range(4):
-        pts[0, q] = feats[:, q, :].astype(jnp.bfloat16)
-    rpts[0] = pts[0, 0]
-
     def shifted(dx, dz):
         return lax.rem(x + dx + SIDE, SIDE) * SIDE + lax.rem(z + dz + SIDE, SIDE)
 
@@ -165,7 +158,18 @@
         pl.semaphore_signal(barrier, inc=1, device_id=(row, shifted(dx, dz)), device_id_type=MESH)
 
     each_peer(greet)
+    local = [pltpu.make_async_copy(points, raw, loc_sem.at[4])]
+    local += [pltpu.make_async_copy(probes.at[q], prb.at[pl.ds(q * OWN, OWN)], loc_sem.at[q]) for q in range(4)]
+    for i, (src, dst) in enumerate(zip(tables, (chosen_leaf, chosen_one, chosen_two, chosen_three))):
+        local.append(pltpu.make_async_copy(src, dst, loc_sem.at[5 + i]))
     for copy in local:
+        copy.start()
+    local[0].wait()
+    feats = raw[...].astype(jnp.float32)
+    for q in range(4):
+        pts[0, q] = feats[:, q, :].astype(jnp.bfloat16)
+    rpts[0] = pts[0, 0]
+    for copy in local[1:]:
         copy.wait()
 
     bits = (lax.rem(col, 2), lax.rem(col // 2, 2))
@@ -181,25 +185,6 @@
             src_ref=src_ref, dst_ref=dst_ref, send_sem=pair_send.at[level, kind], recv_sem=pair_recv.at[level, kind],
             device_id=(row, col + (1 - 2 * bit) * (level + 1)), device_id_type=MESH)
 
-    for leaf in range(2):
-        picks[leaf] = pick_of(chosen_leaf[leaf:leaf + 1, :])
-    picks[2] = pick_of(chosen_one[...])
-    picks[3] = pick_of(chosen_two[pl.ds(col // 2, 1), :])
-    picks[4] = pick_of(chosen_three[pl.ds(col // 4, 1), :])
-
-    def picked(feats, pick):
-        return lax.dot_general(feats, pick, (((1,), (1,)), ((), ())), preferred_element_type=jnp.float32)
-
-    def child_points(level, feats):
-        square[level] = kernel_square(gain, feats)
-        if level < 2:
-            pair_p[level, bits[level]] = picked(feats.astype(jnp.bfloat16), picks[2 + level]).astype(jnp.bfloat16)
-
-    def pair_points(level):
-        pair_copy(level, 0).wait_recv()
-        return jnp.concatenate([pair_p[level, 0], pair_p[level, 1]], axis=1).astype(jnp.float32)
-
-    child_points(0, jnp.concatenate([picked(pts[0, 0, :, leaf * LEAF:(leaf + 1) * LEAF], picks[leaf]) for leaf in range(2)], axis=1))
     pl.semaphore_wait(barrier, 18)
 
     def row_copy(slot, dx, dz):
@@ -231,12 +216,32 @@
     upward(0, 4).start()
     downward(0, 4).start()
     each_peer(lambda slot, dx, dz: row_copy(slot, dx, dz).start())
-    pair_copy(0, 0).start()
     for q in range(4):
         on_chip(0, q).start()
     for q, r in zip((0, 1, 2, 3), (2, 3, 0, 1)):
         upward(0, q).start()
         downward(0, r).start()
+
+    for leaf in range(2):
+        picks[leaf] = pick_of(chosen_leaf[leaf:leaf + 1, :])
+    picks[2] = pick_of(chosen_one[...])
+    picks[3] = pick_of(chosen_two[pl.ds(col // 2, 1), :])
+    picks[4] = pick_of(chosen_three[pl.ds(col // 4, 1), :])
+
+    def picked(feats, pick):
+        return lax.dot_general(feats, pick, (((1,), (1,)), ((), ())), preferred_element_type=jnp.float32)
+
+    def child_points(level, feats):
+        square[level] = kernel_square(gain, feats)
+        if level < 2:
+            pair_p[level, bits[level]] = picked(feats.astype(jnp.bfloat16), picks[2 + level]).astype(jnp.bfloat16)
+
+    def pair_points(level):
+        pair_copy(level, 0).wait_recv()
+        return jnp.concatenate([pair_p[level, 0], pair_p[level, 1]], axis=1).astype(jnp.float32)
+
+    child_points(0, jnp.concatenate([picked(pts[0, 0, :, leaf * LEAF:(leaf + 1) * LEAF], picks[leaf]) for leaf in range(2)], axis=1))
+    pair_copy(0, 0).start()
 
     def col_features(place):
         for q in range(4):
@@ -317,10 +322,10 @@
                 arrived(2, 0, q)
                 on_chip(2, q).start()
 
-        acc[at(4 * i, 4), :] += partial(4 * i, 4, 2, EARLY)
+        acc[at(1 + 3 * i, 3), :] += partial(1 + 3 * i, 3, 2, EARLY)
         return 0
 
-    lax.fori_loop(0, 4, middle, 0)
+    lax.fori_loop(0, 5, middle, 0)
     child_points(2, pair_points(1))
     for dy in (1, 3, 2):
         for q in (4, 0, 1, 2, 3):
@@ -371,7 +376,7 @@
 
     lax.fori_loop(0, 3, far_blocks, 0)
     lax.fori_loop(0, 3, line_blocks, 0)
-    total = acc[at(0, 1), :] + partial(0, 1, EARLY, 8)
+    total = acc[at(0, 1), :] + partial(0, 1, 2, 8)
     for half in range(2):
         summed = half_of(total, half)
         for k in range(3):
@@ -452,22 +457,34 @@
     pltpu.make_async_copy(top_x, top_out, out_sem.at[4]).wait()
 
 
+def finish_kernel(leaf, upper, top, leaf_out, upper_out, top_out):
+    leaf_out[...] = leaf[...]
+    upper_out[...] = upper[...]
+    top_out[...] = top[...]
+
+
 def local(probes, points, leaf_skeleton, skeleton_one, skeleton_two, skeleton_three):
     bf16, f32, dma, vmem = jnp.bfloat16, jnp.float32, pltpu.SemaphoreType.DMA, pltpu.VMEM
     extent = OWN * lax.axis_size("row") * lax.axis_size("col")
     kernel_gain = 16.0 / math.sqrt(4 * extent)
     rows = 16 * OWN
     outside, inside = pl.BlockSpec(memory_space=pl.ANY), pl.BlockSpec(memory_space=vmem)
-    leaf_interp, upper_interp, top_state = pl.pallas_call(
+    outputs = (
+        jax.ShapeDtypeStruct((2, 64, LEAF), f32),
+        jax.ShapeDtypeStruct((3, 64, LEAF), f32),
+        jax.ShapeDtypeStruct((2, 64, 256), f32),
+    )
+    results = pl.pallas_call(
         functools.partial(hss_kernel, kernel_gain),
-        out_shape=(
-            jax.ShapeDtypeStruct((2, 64, LEAF), f32),
-            jax.ShapeDtypeStruct((3, 64, LEAF), f32),
-            jax.ShapeDtypeStruct((2, 64, 256), f32),
-        ),
-        in_specs=[outside, inside, inside, inside, inside, inside],
+        out_shape=outputs,
+        in_specs=[outside] * 6,
         out_specs=(outside, outside, outside),
         scratch_shapes=[
+            vmem((16, 4, OWN), bf16),
+            vmem((2, 64), jnp.int32),
+            vmem((1, 64), jnp.int32),
+            vmem((8, 64), jnp.int32),
+            vmem((4, 64), jnp.int32),
             vmem((8 * CHUNK, 256), bf16),
             vmem((8, 4, 16, OWN), bf16),
             vmem((16, 16, OWN), bf16),
@@ -488,11 +505,13 @@
             vmem((2, 64, LEAF), f32),
             vmem((3, 64, LEAF), f32),
             vmem((2, 64, 256), f32),
-            dma((4,)), dma((16,)), dma((16,)), dma((4, 5)), dma((2, 5)), dma((2, 5)), dma((8, 5)), dma((2, 16)), dma((2, 16)), dma((2, 3)), dma((2, 3)),
+            dma((9,)), dma((16,)), dma((16,)), dma((4, 5)), dma((2, 5)), dma((2, 5)), dma((8, 5)), dma((2, 16)), dma((2, 16)), dma((2, 3)), dma((2, 3)),
             dma((2, 3)), dma((2, 3)), dma((5,)),
         ],
         compiler_params=pltpu.CompilerParams(collective_id=0, has_side_effects=True, vmem_limit_bytes=60 << 20),
     )(probes, points, leaf_skeleton, skeleton_one, skeleton_two, skeleton_three)
+    leaf_interp, upper_interp, top_state = pl.pallas_call(
+        finish_kernel, out_shape=outputs, in_specs=[inside] * 3, out_specs=(inside,) * 3)(*results)
     return leaf_interp.swapaxes(1, 2), upper_interp.swapaxes(1, 2)[:, None], top_state[:, None]
 
 

time: 87.3 us -> 85.4 us (0.978)
  local copies, waits for them, and re-layouts: 2.82 us -> 0 us
  Pallas kernels: 83.6 us -> 84.6 us
    unnamed x7 -> x0, local copies, waits for them, and re-layouts: 2.82 us -> none
    pallas_call x1 -> x2, Pallas kernels: 83.6 us -> 84.6 us  [the longest x1 82.9 us: local(): pl.pallas_call(functools.partial(hss_kernel, kernel_gain), out_shape=outp...]
where the time goes in v5:
time: 85.4 us; the launch traced here: 85.2 us
  Pallas kernels  84.6 us (99%)
    pallas_call x1, Pallas kernels, local(): pl.pallas_call(functools.partial(hss_kernel, kernel_gain), out_shape=outp...  82.9 us

profile of v5, /device:TPU:0, one launch (start us, length us, event | category | flops | bytes accessed | tf_op | source)
XLA Modules:
  0.0 85.2 jit_solution(13405020002724720158)
XLA Ops:
  0.6 82.9 %shard_map.85 = (f32[2,64,128]{2,1,0:T(8,128)}, f32[3,64,128]{2,1,0:T(8,128)}, f32[2,64,256]{2,1,0:T(8,128)}) custom-call(bf16[4,256,256]{2,1,0:T(8,128)(2,1)} %probes.1, bf16[16,4,256]{2,1,0:T(4,128)(2,1)} %points.1, s32[2,64]{1,0:T(2,128)} %table_leaf.1, s32[1,64]{1,0:T(1,128)} %table_one.1, s32[8,64]{1,0:T(8,128)} %table_two.1, s32[4,64]{1,0:T(4,128)} %table_three.1), custom_call_target="tpu_custom_call" | custom-call | tf_op jit(solution)/shard_map/pallas_call | solution.py:477
  83.5 1.7 %shard_map.86 = (f32[2,64,128]{2,1,0:T(8,128)}, f32[3,64,128]{2,1,0:T(8,128)}, f32[2,64,256]{2,1,0:T(8,128)}) custom-call(f32[2,64,128]{2,1,0:T(8,128)} %get-tuple-element.9.leaf, f32[3,64,128]{2,1,0:T(8,128)} %get-tuple-element.10.upper, f32[2,64,256]{2,1,0:T(8,128)} %get-tuple-element.11.top), custom_call_target="tpu_custom_call" | custom-call | tf_op jit(solution)/shard_map/pallas_call | solution.py:513

commit v6 on v5

--- a/solution.py
+++ b/solution.py
@@ -88,21 +88,17 @@
     return [m[:, 64:] for m in systems]
 
 
-def interpolate(stacked, picks, keep=None):
-    systems, kept = [], []
+def interpolate(stacked, skeletons, picks):
+    systems = []
     eye = lax.broadcasted_iota(jnp.int32, (64, 64), 0) == lax.broadcasted_iota(jnp.int32, (64, 64), 1)
-    for y, pick in zip(stacked, picks):
-        z = select_rows(pick, y)
-        kept.append(z)
-        if keep is not None:
-            keep(z)
+    for y, z, pick in zip(stacked, skeletons, picks):
         cross = exact(z, y, ((1,), (1,)))
         gram = lax.dot_general(jnp.concatenate(split(cross), axis=1), jnp.concatenate([pick] * 3, axis=1), (((1,), (1,)), ((), ())), preferred_element_type=jnp.float32)
         diag = jnp.where(eye, gram, 0.0)
         ridge = jnp.sum(diag, keepdims=True) * (0.05 / 64) + 1e-5
         gram = gram + jnp.where(eye, ridge, 0.0)
         systems.append(jnp.concatenate([gram, cross], axis=1))
-    return eliminate(systems), kept
+    return eliminate(systems)
 
 
 def kernel_square(gain, feats):
@@ -390,7 +386,9 @@
     def leave(src, dst, sem):
         pltpu.make_async_copy(src, dst, sem).start()
 
-    solved, kept = interpolate([acc[pl.ds(leaf * LEAF, LEAF), :] for leaf in range(2)], [picks[0], picks[1]])
+    leaves = [acc[pl.ds(leaf * LEAF, LEAF), :] for leaf in range(2)]
+    kept = [select_rows(picks[leaf], leaves[leaf]) for leaf in range(2)]
+    solved = interpolate(leaves, kept, [picks[0], picks[1]])
     reduced = []
     for leaf, value in enumerate(solved):
         rows = prb[pl.ds(leaf * LEAF, LEAF), :]
@@ -405,24 +403,28 @@
             pair_r[level - 1, pl.ds(pl.multiple_of(64 - bits[level - 1] * 64, 64), 64), :] = pair_in[level - 1].astype(jnp.float32)
             below, weights = pair_z[level - 1], pair_r[level - 1]
 
-        def keep(value):
+        rows = below - exact(square[level], weights)
+        skeleton = select_rows(picks[2 + level], rows)
+        half = None if level == 2 else pl.ds(pl.multiple_of(bits[level] * 64, 64), 64)
+        if level == 2:
+            top_x[0] = skeleton
+        else:
+            pair_z[level, half, :] = skeleton
+            pair_copy(level, 1).start()
+
+        @pl.when(row >= 0)
+        def _():
+            (solved,) = interpolate([rows], [skeleton], [picks[2 + level]])
+            value = exact(solved, weights)
             if level == 2:
-                top_x[0] = value
+                top_x[1] = value
+                leave(top_x, top_out, out_sem.at[4])
             else:
-                pair_z[level, pl.ds(pl.multiple_of(bits[level] * 64, 64), 64), :] = value
-                pair_copy(level, 1).start()
-
-        solved, _ = interpolate([below - exact(square[level], weights)], [picks[2 + level]], keep)
-        value = exact(solved[0], weights)
-        if level == 2:
-            top_x[1] = value
-            leave(top_x, top_out, out_sem.at[4])
-        else:
-            pair_out[level] = value.astype(jnp.bfloat16)
-            pair_copy(level, 2).start()
-            pair_r[level, pl.ds(pl.multiple_of(bits[level] * 64, 64), 64), :] = value
-        upper_x[level] = solved[0]
-        leave(upper_x.at[level], upper_out.at[level], out_sem.at[1 + level])
+                pair_out[level] = value.astype(jnp.bfloat16)
+                pair_copy(level, 2).start()
+                pair_r[level, half, :] = value
+            upper_x[level] = solved
+            leave(upper_x.at[level], upper_out.at[level], out_sem.at[1 + level])
 
     def drain(slot, dx, dz):
         row_copy(slot, dx, dz).wait_send()

time: 85.4 us -> 84.2 us (0.986)
  Pallas kernels: 84.6 us -> 83.4 us
    pallas_call x1, Pallas kernels: 82.9 us -> 81.7 us  [local(): pl.pallas_call(functools.partial(hss_kernel, kernel_gain), out_shape=outp...]
where the time goes in v6:
time: 84.2 us; the launch traced here: 84 us
  Pallas kernels  83.4 us (99%)
    pallas_call x1, Pallas kernels, local(): pl.pallas_call(functools.partial(hss_kernel, kernel_gain), out_shape=outp...  81.7 us
    pallas_call x1, Pallas kernels, local(): pl.pallas_call(finish_kernel, out_shape=outputs, in_specs=[inside] * 3, o...  1.7 us

profile of v6, /device:TPU:0, one launch (start us, length us, event | category | flops | bytes accessed | tf_op | source)
XLA Modules:
  0.0 84.0 jit_solution(15799925270929299237)
XLA Ops:
  0.6 81.7 %shard_map.85 = (f32[2,64,128]{2,1,0:T(8,128)}, f32[3,64,128]{2,1,0:T(8,128)}, f32[2,64,256]{2,1,0:T(8,128)}) custom-call(bf16[4,256,256]{2,1,0:T(8,128)(2,1)} %probes.1, bf16[16,4,256]{2,1,0:T(4,128)(2,1)} %points.1, s32[2,64]{1,0:T(2,128)} %table_leaf.1, s32[1,64]{1,0:T(1,128)} %table_one.1, s32[8,64]{1,0:T(8,128)} %table_two.1, s32[4,64]{1,0:T(4,128)} %table_three.1), custom_call_target="tpu_custom_call" | custom-call | tf_op jit(solution)/shard_map/pallas_call | solution.py:479
  82.3 1.7 %shard_map.86 = (f32[2,64,128]{2,1,0:T(8,128)}, f32[3,64,128]{2,1,0:T(8,128)}, f32[2,64,256]{2,1,0:T(8,128)}) custom-call(f32[2,64,128]{2,1,0:T(8,128)} %get-tuple-element.9.leaf, f32[3,64,128]{2,1,0:T(8,128)} %get-tuple-element.10.upper, f32[2,64,256]{2,1,0:T(8,128)} %get-tuple-element.11.top), custom_call_target="tpu_custom_call" | custom-call | tf_op jit(solution)/shard_map/pallas_call | solution.py:515

commit v7 on v6

--- a/solution.py
+++ b/solution.py
@@ -37,7 +37,12 @@
 
 
 def exact(a, b, dims=((1,), (0,))):
-    return lax.dot_general(a, b, (dims, ((), ())), precision=exact_mode, preferred_element_type=jnp.float32)
+    ah, am, _ = split(a)
+    bh, bm, _ = split(b)
+    left = jnp.concatenate([ah, ah, am], axis=1)
+    right = jnp.concatenate([bh, bm, bh], axis=dims[1][0])
+    return lax.dot_general(left, right, (dims, ((), ())), preferred_element_type=jnp.float32)
+
 
 def split(v):
     h = v.astype(jnp.bfloat16)

time: 84.2 us -> 83.2 us (0.988)
  Pallas kernels: 83.4 us -> 82.3 us
    pallas_call x1, Pallas kernels: 81.7 us -> 80.6 us  [local(): pl.pallas_call(functools.partial(hss_kernel, kernel_gain), out_shape=outp...]
where the time goes in v7:
time: 83.2 us; the launch traced here: 83 us
  Pallas kernels  82.3 us (99%)
    pallas_call x1, Pallas kernels, local(): pl.pallas_call(functools.partial(hss_kernel, kernel_gain), out_shape=outp...  80.6 us
    pallas_call x1, Pallas kernels, local(): pl.pallas_call(finish_kernel, out_shape=outputs, in_specs=[inside] * 3, o...  1.7 us

profile of v7, /device:TPU:0, one launch (start us, length us, event | category | flops | bytes accessed | tf_op | source)
XLA Modules:
  0.0 83.0 jit_solution(11410908679033800152)
XLA Ops:
  0.6 80.6 %shard_map.85 = (f32[2,64,128]{2,1,0:T(8,128)}, f32[3,64,128]{2,1,0:T(8,128)}, f32[2,64,256]{2,1,0:T(8,128)}) custom-call(bf16[4,256,256]{2,1,0:T(8,128)(2,1)} %probes.1, bf16[16,4,256]{2,1,0:T(4,128)(2,1)} %points.1, s32[2,64]{1,0:T(2,128)} %table_leaf.1, s32[1,64]{1,0:T(1,128)} %table_one.1, s32[8,64]{1,0:T(8,128)} %table_two.1, s32[4,64]{1,0:T(4,128)} %table_three.1), custom_call_target="tpu_custom_call" | custom-call | tf_op jit(solution)/shard_map/pallas_call | solution.py:484
  81.3 1.7 %shard_map.86 = (f32[2,64,128]{2,1,0:T(8,128)}, f32[3,64,128]{2,1,0:T(8,128)}, f32[2,64,256]{2,1,0:T(8,128)}) custom-call(f32[2,64,128]{2,1,0:T(8,128)} %get-tuple-element.9.leaf, f32[3,64,128]{2,1,0:T(8,128)} %get-tuple-element.10.upper, f32[2,64,256]{2,1,0:T(8,128)} %get-tuple-element.11.top), custom_call_target="tpu_custom_call" | custom-call | tf_op jit(solution)/shard_map/pallas_call | solution.py:520
